TPU v7x, 128 devices: a whole 4x4x4 slice. The times are simulated.
128 devices in a mesh: slab: 16 (over z, x), orb: 8 (over y, core).
Axes of the slice: x: 4, y: 4, z: 4, core: 2. Of those that a mesh axis runs over, the one named last changes fastest.
Arguments:
- orbitals: bfloat16 [4096, 128, 256], P(('slab', 'orb')), may hold values from -12 to 12
- region_start: int32 [4096], P(('slab', 'orb')), may hold values from 0 to 2047, as said below
- kin_cross: bfloat16 [256, 256], replicated, may hold values from -0.375 to 0.375
- potential: float32 [2048, 256], P(('slab', 'orb')), may hold values from 0.5 to 2
- pattern: int32 [64, 5], replicated, may hold values from 0 to 63, as said below
Outputs:
- gradient: bfloat16 [4096, 128, 256], P(('slab', 'orb'))
Inputs may be any that keep to these rules, and one draw needn't show every extreme that they name: `region_start`: region_start_i - (i // 256) * 128 lies in 0 to 127 and takes both ends within every slab's orbitals; regions continue periodically past the last grid column. `pattern`: row b lists 5 distinct blocks, b among them, all whose orbitals begin in slab b // 4 or the slab before or after it, taken periodically.
All inputs are finite; a program needn't handle non-finite values.
Results may differ from a plain program's by a relative error of at most 0.0085.
Values may be sent and summed in bfloat16 or wider, within the bound.
No kernel may reach another device: no remote copies, remote signals or barrier semaphores. Data moves between devices by JAX's collectives and lax.ppermute only.
A program may use at most 128 MiB of HBM per device.

v0:
```python
import functools
import jax
import jax.numpy as jnp
from jax import lax
from jax.experimental import pallas as pl
from jax.experimental.pallas import tpu as pltpu
from jax.sharding import PartitionSpec as P

BLOCK = 64
CUTS = (0, 2, 4)
F32 = jnp.float32
BF16 = jnp.bfloat16
PARTIAL = BF16
NT = (((1,), (1,)), ((), ()))


def params():
    return pltpu.CompilerParams(vmem_limit_bytes=56 * 1024 * 1024)


def smem():
    return pl.BlockSpec(memory_space=pltpu.SMEM)


def fixed(*shape):
    return pl.BlockSpec(shape, lambda t: (0,) * len(shape))


def shaped(shape, dtype=BF16):
    return jax.ShapeDtypeStruct(shape, dtype)


def other_core(place_ref, side):
    return place_ref[4] if side == 0 else 1 - place_ref[4]


def spread_kernel(start_ref, place_ref, x_ref, *rest, cuts):
    outs, scratch = rest[:-1], rest[-1]
    held, length, cross = x_ref.shape
    levels = 4
    narrow = length // (2 * levels)
    base = place_ref[1] * length
    gap = (
        lax.broadcasted_iota(jnp.int32, (length, length), 0)
        - lax.broadcasted_iota(jnp.int32, (length, length), 1)
    ) & (length - 1)
    which_row = lax.broadcasted_iota(jnp.int32, (held, cross), 0)
    offsets = jnp.zeros((held, cross), jnp.int32)
    for j in range(held):
        offset = start_ref[pl.program_id(0) * held + j] - base
        offsets = jnp.where(which_row == j, offset, offsets)
        shift = (offset + length // 2) & (length - 1)
        pick = jnp.where(gap == shift, 1.0, 0.0).astype(BF16)
        rolled = jnp.dot(pick, x_ref[j], preferred_element_type=F32)
        for half in range(cross // 128):
            scratch[half, pl.ds(j, length, stride=held), :] = rolled[:, half * 128 : half * 128 + 128]
    offsets = offsets.astype(F32).astype(BF16)
    for d in range(levels):
        for side in range(2):
            group = other_core(place_ref, side) * levels + ((place_ref[3] + d) & (levels - 1))
            outs[d][side, 0] = offsets
            for which, (first, last) in enumerate(spans(cuts)):
                for q in range(first, last):
                    row = (group * narrow + q - 1) & (length - 1)
                    to = q - first + (1 if which == 0 else 0)
                    for half in range(cross // 128):
                        outs[which * levels + d][side, to, :, half * 128 : half * 128 + 128] = scratch[
                            half, pl.ds(pl.multiple_of(row * held, held), held), :
                        ].astype(BF16)


def spans(cuts):
    return [
        (0 if i == 0 else 4 * cuts[i] + 2, 4 * cuts[i + 1] + 2) for i in range(len(cuts) - 1)
    ]


def collect_kernel(start_ref, place_ref, *rest, cuts):
    levels = 4
    out_ref, scratch = rest[-2], rest[-1]
    held, length, cross = out_ref.shape
    narrow = length // (2 * levels)
    base = place_ref[1] * length + length // 2
    gap = (
        lax.broadcasted_iota(jnp.int32, (length, length), 1)
        - lax.broadcasted_iota(jnp.int32, (length, length), 0)
    ) & (length - 1)
    for which in range(len(cuts) - 1):
        wide = 4 * (cuts[which + 1] - cuts[which])
        for d in range(levels):
            for side in range(2):
                group = other_core(place_ref, side) * levels + ((place_ref[3] - d) & (levels - 1))
                first = (group * narrow + 4 * cuts[which]) * held
                for half in range(cross // 128):
                    scratch[half, pl.ds(pl.multiple_of(first, 4 * held), wide * held), :] = (
                        rest[which * levels + d][side, :, :, half * 128 : half * 128 + 128]
                        .reshape(wide * held, 128)
                        .astype(F32)
                    )
    for j in range(held):
        shift = (start_ref[pl.program_id(0) * held + j] - base) & (length - 1)
        pick = jnp.where(gap == shift, 1.0, 0.0).astype(BF16)
        rows = jnp.concatenate(
            [scratch[half, pl.ds(j, length, stride=held), :] for half in range(cross // 128)], axis=1
        ).astype(BF16)
        out_ref[j] = jnp.dot(pick, rows, preferred_element_type=F32).astype(BF16)


def make_fields(place_ref, pot_ref, kin_ref, off_ref, row_at, across_ref, phi_ref, app_ref, *, own, start):
    cross = kin_ref.shape[0]
    quads, count, _ = phi_ref.shape
    levels = 4
    held = count // (2 * levels)
    units = [(d, side) for d in range(levels) for side in range(2)]
    places = [
        pl.multiple_of(
            (((place_ref[3] - d) & (levels - 1)) * 2 + other_core(place_ref, side)) * held, held
        )
        for d, side in units
    ]
    for col in range(4 * quads):
        lanes = slice((col % 4) * cross, (col % 4 + 1) * cross)
        now = start * 4 + col
        for (d, side), at in zip(units, places):
            place = place_ref[0] + now - off_ref[pl.ds(at, held), :].astype(jnp.int32)
            inside = (place >= 0) & (place < 128)
            keep = jnp.where(inside, 1.0, 0.0) if own else jnp.where(inside, 0.0, 1.0)
            keep = jnp.concatenate([keep, keep], axis=1)
            phi_ref[col // 4, pl.ds(at, held), lanes] = (
                row_at(side, d, now + 1).astype(F32) * keep
            ).astype(BF16)
        across_ref[...] = jnp.dot(
            phi_ref[col // 4, :, lanes], kin_ref[...], preferred_element_type=F32
        )
        for (d, side), at in zip(units, places):
            place = place_ref[0] + now - off_ref[pl.ds(at, held), :].astype(jnp.int32)
            inside = (place >= 0) & (place < 128)
            keep = jnp.where(inside, 0.5, 0.0) if own else jnp.where(inside, 0.0, 0.5)
            row = place & 127
            left = jnp.where(row == 0, 0.0, keep)
            right = jnp.where(row == 127, 0.0, keep)
            left = jnp.concatenate([left, left], axis=1)
            right = jnp.concatenate([right, right], axis=1)
            phi = phi_ref[col // 4, pl.ds(at, held), lanes].astype(F32)
            around = row_at(side, d, now).astype(F32) * left + row_at(side, d, now + 2).astype(F32) * right
            kin = (phi - around + across_ref[pl.ds(at, held), :]).astype(BF16).astype(F32)
            app_ref[col // 4, pl.ds(at, held), lanes] = (
                kin + pot_ref[now : now + 1, :] * phi
            ).astype(BF16)


def chunk_inputs(refs, which, cuts):
    if which == 0:
        pair, rest = refs[:2], refs[2:]

        def row_at(side, d, q):
            return pair[side][d, q + 1]

        return row_at, rest
    pair, edges, rest = refs[:2], refs[2:6], refs[6:]
    first = spans(cuts)[which][0]

    def row_at(side, d, q):
        if q >= first:
            return pair[side][d, q - first]
        return edges[2 * side + q - first + 2][d, 0]

    return row_at, rest


def own_kernel(place_ref, pot_ref, kin_ref, *refs, which, cuts):
    row_at, rest = chunk_inputs(refs, which, cuts)
    if which == 0:
        phi_ref, app_ref, pair_ref, off_ref, across_ref = rest
        store_offsets(place_ref, refs, off_ref)
    else:
        off_ref, before_ref, phi_ref, app_ref, pair_ref, across_ref = rest
    make_fields(
        place_ref, pot_ref, kin_ref, off_ref, row_at, across_ref, phi_ref, app_ref,
        own=True, start=cuts[which],
    )
    for quad in range(phi_ref.shape[0]):
        phi = phi_ref[quad]
        both = jnp.concatenate([phi, app_ref[quad]], axis=0)
        term = lax.dot_general(both, phi, NT, preferred_element_type=F32)
        if quad > 0:
            pair_ref[...] += term
        elif which == 0:
            pair_ref[...] = term
        else:
            pair_ref[...] = before_ref[...] + term


def store_offsets(place_ref, refs, off_ref):
    levels, _, held, _ = refs[0].shape
    for side in range(2):
        for d in range(levels):
            unit = ((place_ref[3] - d) & (levels - 1)) * 2 + other_core(place_ref, side)
            off_ref[pl.ds(pl.multiple_of(unit * held, held), held), :] = refs[side][d, 0][:, :128].astype(F32)


def near_kernel(place_ref, pattern_ref, pot_ref, kin_ref, *refs, which, cuts, scale):
    row_at, rest = chunk_inputs(refs, which, cuts)
    last = which == len(cuts) - 2
    phi_own_ref, app_own_ref, rest = rest[0], rest[1], rest[2:]
    if last:
        pair_ref, rest = rest[0], rest[1:]
    if which == 0:
        phi_ref, app_ref, off_ref, rest = rest[0], rest[1], rest[2], rest[3:]
        store_offsets(place_ref, refs, off_ref)
    else:
        off_ref, before_ref, phi_ref, app_ref, rest = rest[0], rest[1], rest[2], rest[3], rest[4:]
    if last:
        outs, table, across_ref = rest[:4], rest[4], rest[5]
    else:
        table, across_ref = rest
    make_fields(
        place_ref, pot_ref, kin_ref, off_ref, row_at, across_ref, phi_ref, app_ref,
        own=False, start=cuts[which],
    )
    count = phi_ref.shape[1]
    for quad in range(phi_ref.shape[0]):
        phi_own, app_own, phi, app = phi_own_ref[quad], app_own_ref[quad], phi_ref[quad], app_ref[quad]
        every = jnp.concatenate([phi_own, phi, app_own, app], axis=0)
        near = lax.dot_general(every, phi, NT, preferred_element_type=F32)
        both = jnp.concatenate([phi, app], axis=0)
        home = lax.dot_general(both, phi_own, NT, preferred_element_type=F32)
        for kind in range(2):
            right = near[kind * 2 * count : (kind + 1) * 2 * count]
            left = home[kind * count : (kind + 1) * count]
            if quad > 0:
                table[kind, : 2 * count, count:] += right
                table[kind, count : 2 * count, :count] += left
            elif which > 0:
                table[kind, : 2 * count, count:] = right + before_ref[kind, : 2 * count, count:]
                table[kind, count : 2 * count, :count] = (
                    left + before_ref[kind, count : 2 * count, :count]
                )
            else:
                table[kind, : 2 * count, count:] = right
                table[kind, count : 2 * count, :count] = left
    if not last:
        return
    for kind in range(2):
        table[kind, :count, :count] = pair_ref[kind * count : (kind + 1) * count]
        table[kind, 2 * count :, :] = jnp.zeros_like(table[kind, 2 * count :, :])
    low = lax.broadcasted_iota(jnp.int32, (16, 128), 1) < BLOCK
    per_slab = count // BLOCK
    for group in range(2 * count // 128):
        for slot in range(5):
            first, second = [
                local_block(place_ref, pattern_ref, 2 * group + side, slot, per_slab) * BLOCK
                for side in range(2)
            ]
            for by in range(4):
                quarter = ((place_ref[3] + by) & 3) * 16
                for kind in range(2):
                    lanes = slice(group * 128, group * 128 + 128)
                    one = table[kind, pl.ds(pl.multiple_of(first + quarter, 16), 16), lanes]
                    two = table[kind, pl.ds(pl.multiple_of(second + quarter, 16), 16), lanes]
                    outs[by][kind, slot * 16 : slot * 16 + 16, lanes] = (
                        jnp.where(low, one, two) * scale
                    ).astype(outs[by].dtype)


def local_block(place_ref, pattern_ref, block, slot, per_slab):
    home, near = place_ref[1], place_ref[2]
    base = home if block < per_slab else near
    listed = pattern_ref[base * per_slab + block % per_slab, slot]
    slab = listed // per_slab
    inner = listed % per_slab
    return jnp.where(slab == home, inner, jnp.where(slab == near, per_slab + inner, 2 * per_slab))


def unpack_kernel(place_ref, pattern_ref, home_ref, near_ref, out_ref):
    total = out_ref.shape[0]
    per_slab = total // 2 // BLOCK
    low = lax.broadcasted_iota(jnp.int32, (16, 128), 1) < BLOCK
    for group in range(total // 128):
        parts = home_ref if group < total // 256 else near_ref
        first = group * 128 % (total // 2)
        lanes = slice(first, first + 128)
        found = []
        for slot in range(5):
            first, second = [
                local_block(place_ref, pattern_ref, 2 * group + side, slot, per_slab)
                for side in range(2)
            ]
            found.append(jnp.where(low, first, second))
        for block in range(2 * per_slab):
            hits = [jnp.where(found[slot] == block, 1.0, 0.0) for slot in range(5)]
            for by in range(4):
                quarter = (place_ref[3] - by) & 3
                side = (quarter // 2) ^ place_ref[4]
                d = (block % per_slab - place_ref[3]) & 3
                row = ((block // per_slab * 2 + side) * 4 + d) * 32 + (quarter % 2) * 16
                for kind in range(2):
                    acc = jnp.zeros((16, 128), F32)
                    for slot in range(5):
                        part = parts[by, kind, slot * 16 : slot * 16 + 16, lanes].astype(F32)
                        acc = acc + part * hits[slot]
                    if kind == 1:
                        acc = -acc
                    out_ref[
                        pl.ds(pl.multiple_of(row, 16), 16),
                        kind * total + group * 128 : kind * total + group * 128 + 128,
                    ] = acc.astype(BF16)


def gradient_kernel(place_ref, off_own_ref, off_near_ref, mat_ref, *rest, start, scale):
    ins, outs = rest[:4], rest[4:]
    levels, _, held, cross = outs[0].shape
    phi_own_ref, app_own_ref, phi_ref, app_ref = ins
    seats = []
    for ref in (off_own_ref, off_near_ref):
        for side in range(2):
            for d in range(levels):
                unit = ((place_ref[3] + d) & (levels - 1)) * 2 + other_core(place_ref, side)
                seats.append(
                    ref[pl.ds(pl.multiple_of(unit * held, held), held), :].astype(jnp.int32)
                )
    right = jnp.concatenate([app_own_ref[0], app_ref[0], phi_own_ref[0], phi_ref[0]], axis=0)
    grad = jnp.dot(mat_ref[...], right, preferred_element_type=F32)
    base = place_ref[0] + start * 4 + pl.program_id(0) * 4
    for step in range(4):
        for i, seat in enumerate(seats):
            place = base + step - seat
            inside = (place >= 0) & (place < 128)
            own = i < 2 * levels
            keep = jnp.where(inside, scale, 0.0) if own else jnp.where(inside, 0.0, scale)
            keep = jnp.concatenate([keep, keep], axis=1)
            part = grad[i * held : (i + 1) * held, step * cross : (step + 1) * cross] * keep
            outs[i // levels][i % levels, step] = part.astype(BF16)


def body(orbitals, region_start, kin_cross, potential, pattern):
    held, length, cross = orbitals.shape
    peers = lax.axis_size("orb")
    slabs = lax.axis_size("slab")
    slab_id = lax.axis_index("slab").astype(jnp.int32)
    orb_id = lax.axis_index("orb").astype(jnp.int32)
    core, level = orb_id % 2, orb_id // 2
    levels = peers // 2
    count = held * peers
    narrow = length // peers
    axes = ("slab", "orb")
    cuts = CUTS
    chunks = len(cuts) - 1

    def send(array, route):
        pairs = []
        for s in range(slabs):
            for k in range(peers):
                ds, dk = route(k % 2, k // 2)
                pairs.append((s * peers + k, ((s + ds) % slabs) * peers + dk))
        return lax.ppermute(array, axes, pairs)

    def onward(array):
        return send(array, lambda c, y: ((1, 2 * y) if c == 0 else (-1, 2 * y + 1)))

    def back(array):
        return send(array, lambda c, y: ((-1, 2 * y) if c == 0 else (1, 2 * y + 1)))

    def across_up(array):
        return send(array, lambda c, y: ((-1, 2 * y + 1) if c == 0 else (1, 2 * y)))

    def swapped(array):
        return send(array, lambda c, y: (0, 2 * y + 1 - c))

    def around(array, by):
        return send(array, lambda c, y: (0, 2 * ((y + by) % levels) + c))

    near_id = jnp.where(core == 0, slab_id - 1, slab_id + 1) % slabs
    position = (core * levels + level) * narrow + length // 2
    place = jnp.stack([position, slab_id, near_id, level, core])

    pot_pairs = []
    for s in range(slabs):
        for k in range(peers):
            if k >= levels:
                pot_pairs.append((s * peers + k, s * peers + 2 * (k - levels)))
            else:
                pot_pairs.append((s * peers + k, ((s - 1) % slabs) * peers + 2 * k + 1))
    window_pot = lax.ppermute(potential, axes, pot_pairs)

    def call(kernel, outs, ins, args, scratch=(), smems=0, **extra):
        return pl.pallas_call(
            kernel,
            grid=(1,),
            out_shape=outs,
            in_specs=[smem()] * smems + ins,
            out_specs=jax.tree.map(lambda item: fixed(*item.shape), outs),
            scratch_shapes=list(scratch),
            compiler_params=params(),
            **extra,
        )(*args)

    def whole(arrays):
        return [fixed(*item.shape) for item in arrays]

    part = held // 2
    scratch = pltpu.VMEM((cross // 128, length * part, 128), F32)
    deep = [last - first + (1 if i == 0 else 0) for i, (first, last) in enumerate(spans(cuts))]
    by_part = pl.BlockSpec((part, length, cross), lambda t: (t, 0, 0))
    pieces = pl.pallas_call(
        functools.partial(spread_kernel, cuts=cuts),
        grid=(2,),
        out_shape=[shaped((2, rows, held, cross)) for rows in deep for _ in range(levels)],
        in_specs=[smem(), smem(), by_part],
        out_specs=[
            pl.BlockSpec((2, rows, part, cross), lambda t: (0, 0, t, 0))
            for rows in deep
            for _ in range(levels)
        ],
        scratch_shapes=[scratch],
        compiler_params=params(),
        name="spread",
    )(region_start, place, orbitals)
    across = pltpu.VMEM((count, cross), F32)
    home_sides, near_sides = [], []
    for which in range(chunks):
        mine = pieces[which * levels : (which + 1) * levels]
        got = [mine[0]] + [around(mine[by], by) for by in range(1, levels)]
        same = jnp.stack([item[0] for item in got])
        other = jnp.stack([item[1] for item in got])
        near_sides.append((onward(same), across_up(other)))
        home_sides.append((same, swapped(other)))

    def chunk_args(sides, which):
        arrays = list(sides[which])
        specs = whole(arrays)
        if which > 0:
            for side in range(2):
                for back_by in (2, 1):
                    item = sides[which - 1][side]
                    at = item.shape[1] - back_by
                    arrays.append(item)
                    specs.append(
                        pl.BlockSpec(
                            (levels, 1, held, cross), lambda t, at=at: (0, at, 0, 0)
                        )
                    )
        return arrays, specs

    fields = [
        shaped((cuts[i + 1] - cuts[i], count, 4 * cross)) for i in range(chunks)
    ]
    seat = shaped((count, 128), F32)
    homes, nears = [], []
    home_off = near_off = pair = table = None
    for which in range(chunks):
        arrays, specs = chunk_args(home_sides, which)
        fixed_args = [window_pot, kin_cross]
        outs = [fields[which]] * 2 + [shaped((2 * count, count), F32)]
        if which == 0:
            outs.append(seat)
            more = []
        else:
            more = [home_off, pair]
        result = call(
            functools.partial(own_kernel, which=which, cuts=cuts),
            outs,
            whole(fixed_args) + specs + whole(more),
            (place, *fixed_args, *arrays, *more),
            [across],
            1,
        )
        homes.append(result[:2])
        pair = result[2]
        if which == 0:
            home_off = result[3]
    packed = (2, 5 * 16, 2 * count)
    table_shape = (2, 2 * count + BLOCK, 2 * count)
    for which in range(chunks):
        arrays, specs = chunk_args(near_sides, which)
        fixed_args = [window_pot, kin_cross]
        last = which == chunks - 1
        more = list(homes[which])
        if last:
            more.append(pair)
        outs = [fields[which]] * 2
        if which == 0:
            outs.append(seat)
        else:
            more += [near_off, table]
        if last:
            outs += [shaped(packed, PARTIAL)] * 4
            temp = [pltpu.VMEM(table_shape, F32), across]
        else:
            outs += [shaped((2, 2 * count, 2 * count), F32)]
            temp = [across]
        result = call(
            functools.partial(near_kernel, which=which, cuts=cuts, scale=1.0 / (length * cross)),
            outs,
            whole(fixed_args) + specs + whole(more),
            (place, pattern, *fixed_args, *arrays, *more),
            temp,
            2,
        )
        nears.append(result[:2])
        rest = result[2:]
        if which == 0:
            near_off, rest = rest[0], rest[1:]
        if last:
            parts = rest
        else:
            table = rest[0]

    total = parts[0].astype(F32)
    for item in [around(parts[by], by) for by in range(1, levels)]:
        total = total + item.astype(F32)
    held_sum = total[:, :, :count] + back(total[:, :, count:].astype(PARTIAL)).astype(F32)
    done = (held_sum + swapped(held_sum)).astype(BF16)
    dones = jnp.stack([done] + [around(done, by) for by in range(1, levels)])
    passed = onward(dones)
    mat = call(
        unpack_kernel,
        shaped((2 * count, 4 * count)),
        whole([dones, passed]),
        (place, pattern, dones, passed),
        (),
        2,
    )
    got = []
    for which in range(chunks):
        wide = 4 * (cuts[which + 1] - cuts[which])
        more = [home_off, near_off, mat, *homes[which], *nears[which]]
        by_quad = pl.BlockSpec((1, count, 4 * cross), lambda t: (t, 0, 0))
        own_same, own_other, near_same, near_other = pl.pallas_call(
            functools.partial(
                gradient_kernel, start=cuts[which], scale=1.0 / (pattern.shape[1] * BLOCK)
            ),
            grid=(wide // 4,),
            out_shape=[shaped((levels, wide, held, cross))] * 4,
            in_specs=[smem()] + whole(more[:3]) + [by_quad] * 4,
            out_specs=[pl.BlockSpec((levels, 4, held, cross), lambda t: (0, t, 0, 0))] * 4,
            compiler_params=params(),
        )(place, *more)
        first, second = back(near_same), across_up(near_other)
        given = swapped(own_other)
        first = own_same + first
        second = given + second
        mine = [jnp.stack([first[d], second[d]]) for d in range(levels)]
        got += [mine[0]] + [around(mine[by], by) for by in range(1, levels)]
    return pl.pallas_call(
        functools.partial(collect_kernel, cuts=cuts),
        grid=(2,),
        out_shape=shaped(orbitals.shape),
        in_specs=[smem(), smem()]
        + [pl.BlockSpec((2, item.shape[1], part, cross), lambda t: (0, 0, t, 0)) for item in got],
        out_specs=by_part,
        scratch_shapes=[scratch],
        compiler_params=params(),
        name="collect",
    )(region_start, place, *got)


def solution(mesh):
    placed = (
        P(("slab", "orb"), None, None),
        P(("slab", "orb")),
        P(),
        P(("slab", "orb"), None),
        P(),
    )
    return jax.shard_map(
        body,
        mesh=mesh,
        in_specs=placed,
        out_specs=P(("slab", "orb"), None, None),
        check_vma=False,
    )
```

profile of v0, /device:TPU:1, one launch (start us, length us, event | category | flops | bytes accessed | tf_op | source)
XLA Modules:
  0.0 190.5 jit_solution(11355590076009575085)
XLA Ops:
  0.0 7.8 %collective-permute-start = (f32[16,256]{1,0:T(8,128)}, f32[16,256]{1,0:T(8,128)S(1)}, u32[]{:S(2)}, u32[]{:S(2)}) collective-permute-start(f32[16,256]{1,0:T(8,128)} %param.8), channel_id=1, source_target_pairs={{0,121},{1,123},{2,125},{3,127},{4,0},{5,2},{6,4},{7,6},{8,1},{9,3... | collective-permute-start | bytes 49160 | tf_op jit(solution)/shard_map/ppermute | solution.py:384
  7.8 0.6 stack.74.place_ref
  8.4 4.6 %spread.1 = (bf16[2,11,32,256]{3,2,1,0:T(8,128)(2,1)}, bf16[2,11,32,256]{3,2,1,0:T(8,128)(2,1)}, bf16[2,11,32,256]{3,2,1,0:T(8,128)(2,1)}, bf16[2,11,32,256]{3,2...) custom-call(s32[32]{0:T(128)} %start_ref.3, ...), custom_call_target="tpu_custom_call" | custom-call | tf_op jit(solution)/shard_map/spread/pallas_call | solution.py:405
  13.0 2.1 %collective-permute-start.7 = (bf16[2,8,32,256]{3,2,1,0:T(8,128)(2,1)}, bf16[2,8,32,256]{3,2,1,0:T(8,128)(2,1)S(1)}, u32[]{:S(2)}, u32[]{:S(2)}) collective-permute-start(bf16[2,8,32,256]{3,2,1,0:T(8,128)(2,1)} %get-tuple-element.47), channel_id=1, source_target_pairs={{0,2},{1,3},{2,4},{3,5},{4,6},{5,7},{6,0},{7,1},{8,10},{9,11},{10,... | collective-permute-start | bytes 786440 | tf_op jit(solution)/shard_map/ppermute | solution.py:356
  15.0 2.5 %collective-permute-start.9 = (bf16[2,8,32,256]{3,2,1,0:T(8,128)(2,1)}, bf16[2,8,32,256]{3,2,1,0:T(8,128)(2,1)S(1)}, u32[]{:S(2)}, u32[]{:S(2)}) collective-permute-start(bf16[2,8,32,256]{3,2,1,0:T(8,128)(2,1)} %get-tuple-element.49), channel_id=1, source_target_pairs={{0,6},{1,7},{2,0},{3,1},{4,2},{5,3},{6,4},{7,5},{8,14},{9,15},{10,... | collective-permute-start | bytes 786440 | tf_op jit(solution)/shard_map/ppermute | solution.py:356
  17.5 1.0 fusion.4
  18.6 1.0 fusion.8
  19.5 8.8 %collective-permute-done.7 = bf16[2,8,32,256]{3,2,1,0:T(8,128)(2,1)S(1)} collective-permute-done((bf16[2,8,32,256]{3,2,1,0:T(8,128)(2,1)}, bf16[2,8,32,256]{3,2,1,0:T(8,128)(2,1)S(1)}, u32[]{:S(2)}, u32[]{:S(2)}) %collective-permute-start.7) | collective-permute-done | bytes 262176 | tf_op jit(solution)/shard_map/ppermute | solution.py:356
  28.4 15.1 %collective-permute-done.1 = bf16[2,11,32,256]{3,2,1,0:T(8,128)(2,1)S(1)} collective-permute-done((bf16[2,11,32,256]{3,2,1,0:T(8,128)(2,1)}, bf16[2,11,32,256]{3,2,1,0:T(8,128)(2,1)S(1)}, u32[]{:S(2)}, u32[]{:S(2)}) %collective-permute-start.1) | collective-permute-done | bytes 360480 | tf_op jit(solution)/shard_map/ppermute | solution.py:356
  43.6 9.7 %collective-permute-done.3 = bf16[2,11,32,256]{3,2,1,0:T(8,128)(2,1)S(1)} collective-permute-done((bf16[2,11,32,256]{3,2,1,0:T(8,128)(2,1)}, bf16[2,11,32,256]{3,2,1,0:T(8,128)(2,1)S(1)}, u32[]{:S(2)}, u32[]{:S(2)}) %collective-permute-start.3) | collective-permute-done | bytes 360480 | tf_op jit(solution)/shard_map/ppermute | solution.py:356
  53.3 0.9 pad_maximum_fusion.1
  54.3 1.3 collective-permute-start.4
  55.6 0.1 collective-permute-start.6
  55.7 0.1 pad_maximum_fusion.refs_0_.refs_2_.refs_3_
  55.8 4.7 %collective-permute-start.5 = (bf16[4,11,32,256]{3,2,1,0:T(8,128)(2,1)S(1)}, bf16[4,11,32,256]{3,2,1,0:T(8,128)(2,1)S(1)}, u32[]{:S(2)}, u32[]{:S(2)}) collective-permute-start(bf16[4,11,32,256]{3,2,1,0:T(8,128)(2,1)S(1)} %pad_maximum_fusion.refs_0_.refs_2_.refs_3_), channel_id=1, source_target_pairs={{0,8},{1,121},{2,10},{3,123},{4,12},{5,125},{6,14},{7,127},{8,16},... | collective-permute-start | bytes 2162696 | tf_op jit(solution)/shard_map/ppermute | solution.py:356
  60.5 0.8 pad_maximum_fusion.3
  61.5 0.5 collective-permute-start.10
  62.0 0.8 copy.6.pattern_ref
  62.9 5.2 %shard_map.55 = (bf16[2,256,1024]{2,1,0:T(8,128)(2,1)}, bf16[2,256,1024]{2,1,0:T(8,128)(2,1)}, f32[512,256]{1,0:T(8,128)}, f32[256,128]{1,0:T(8,128)}) custom-call(s32[5]{0:T(128)} %stack.74.place_ref, f32[16,256]{1,0:T(8,128)} %copy-done.9, bf16[256,256]{1,0:T(8,128)(2,1)} %kin_ref.7, bf16[4,11,32,256]{3,2,1,0:T(8,128)(2,1)} %copy-done, ...), custom_call_target="tpu_custom_call" | custom-call | tf_op jit(solution)/shard_map/pallas_call | solution.py:387
  68.0 5.2 %shard_map.57 = (bf16[2,256,1024]{2,1,0:T(8,128)(2,1)}, bf16[2,256,1024]{2,1,0:T(8,128)(2,1)}, f32[512,256]{1,0:T(8,128)}) custom-call(s32[5]{0:T(128)} %stack.74.place_ref, f32[16,256]{1,0:T(8,128)} %copy-done.9, bf16[256,256]{1,0:T(8,128)(2,1)} %kin_ref.7, bf16[4,8,32,256]{3,2,1,0:T(8,128)(2,1)} %copy-done.4, ...), custom_call_target="tpu_custom_call" | custom-call | tf_op jit(solution)/shard_map/pallas_call | solution.py:387
  73.2 3.3 %collective-permute-done.5.refs_0_.refs_2_.refs_3_ = bf16[4,11,32,256]{3,2,1,0:T(8,128)(2,1)S(1)} collective-permute-done((bf16[4,11,32,256]{3,2,1,0:T(8,128)(2,1)S(1)}, bf16[4,11,32,256]{3,2,1,0:T(8,128)(2,1)S(1)}, u32[]{:S(2)}, u32[]{:S(2)}) %collective-permute-start.5) | collective-permute-done | bytes 720928 | tf_op jit(solution)/shard_map/ppermute | solution.py:356
  76.5 0.9 copy-done.3
  77.4 0.3 copy-done.2
  77.6 7.1 %shard_map.56 = (bf16[2,256,1024]{2,1,0:T(8,128)(2,1)}, bf16[2,256,1024]{2,1,0:T(8,128)(2,1)}, f32[256,128]{1,0:T(8,128)}, f32[2,512,512]{2,1,0:T(8,128)}) custom-call(s32[5]{0:T(128)} %stack.74.place_ref, s32[64,5]{1,0:T(8,128)} %copy.6.pattern_ref, f32[16,256]{1,0:T(8,128)} %copy-done.9, bf16[256,256]{1,0:T(8,128)(2,1)} %kin_ref.7, ...), custom_call_target="tpu_custom_call" | custom-call | tf_op jit(solution)/shard_map/pallas_call | solution.py:387
  84.7 0.1 collective-permute-done.10.refs_0_
  84.8 0.6 collective-permute-done.11.refs_1_
  85.4 8.5 %shard_map.58 = (bf16[2,256,1024]{2,1,0:T(8,128)(2,1)}, bf16[2,256,1024]{2,1,0:T(8,128)(2,1)}, bf16[2,80,512]{2,1,0:T(8,128)(2,1)}, bf16[2,80,512]{2,1,0:T(8,128...) custom-call(s32[5]{0:T(128)} %stack.74.place_ref, s32[64,5]{1,0:T(8,128)} %copy.6.pattern_ref, ...), custom_call_target="tpu_custom_call" | custom-call | tf_op jit(solution)/shard_map/pallas_call | solution.py:387
  93.9 2.4 %collective-permute-start.14 = (bf16[2,80,512]{2,1,0:T(8,128)(2,1)}, bf16[2,80,512]{2,1,0:T(8,128)(2,1)S(1)}, u32[]{:S(2)}, u32[]{:S(2)}) collective-permute-start(bf16[2,80,512]{2,1,0:T(8,128)(2,1)} %get-tuple-element.57), channel_id=1, source_target_pairs={{0,4},{1,5},{2,6},{3,7},{4,0},{5,1},{6,2},{7,3},{8,12},{9,13},{10,... | collective-permute-start | bytes 491528 | tf_op jit(solution)/shard_map/ppermute | solution.py:356
  96.3 0.3 collective-permute-start.15
  96.6 4.7 %collective-permute-done.13 = bf16[2,80,512]{2,1,0:T(8,128)(2,1)S(1)} collective-permute-done((bf16[2,80,512]{2,1,0:T(8,128)(2,1)}, bf16[2,80,512]{2,1,0:T(8,128)(2,1)S(1)}, u32[]{:S(2)}, u32[]{:S(2)}) %collective-permute-start.13) | collective-permute-done | bytes 163872 | tf_op jit(solution)/shard_map/ppermute | solution.py:356
  101.2 0.9 collective-permute-done.15
  102.2 1.0 convert_add_fusion
  103.3 8.6 %collective-permute-done.16 = bf16[2,80,256]{2,1,0:T(8,128)(2,1)S(1)} collective-permute-done((bf16[2,80,256]{2,1,0:T(8,128)(2,1)S(1)}, bf16[2,80,256]{2,1,0:T(8,128)(2,1)S(1)}, u32[]{:S(2)}, u32[]{:S(2)}) %collective-permute-start.16) | collective-permute-done | bytes 81952 | tf_op jit(solution)/shard_map/ppermute | solution.py:356
  111.8 0.7 collective-permute-start.17
  112.6 1.0 collective-permute-done.17
  113.6 2.3 %collective-permute-start.20 = (bf16[2,80,256]{2,1,0:T(8,128)(2,1)S(1)}, bf16[2,80,256]{2,1,0:T(8,128)(2,1)S(1)}, u32[]{:S(2)}, u32[]{:S(2)}) collective-permute-start(bf16[2,80,256]{2,1,0:T(8,128)(2,1)S(1)} %add_convert_fusion), channel_id=1, source_target_pairs={{0,6},{1,7},{2,0},{3,1},{4,2},{5,3},{6,4},{7,5},{8,14},{9,15},{10,... | collective-permute-start | bytes 245768 | tf_op jit(solution)/shard_map/ppermute | solution.py:356
  115.9 0.7 collective-permute-start.18
  116.6 1.2 collective-permute-done.20
  117.7 3.1 %collective-permute-done.19 = bf16[2,80,256]{2,1,0:T(8,128)(2,1)S(1)} collective-permute-done((bf16[2,80,256]{2,1,0:T(8,128)(2,1)S(1)}, bf16[2,80,256]{2,1,0:T(8,128)(2,1)S(1)}, u32[]{:S(2)}, u32[]{:S(2)}) %collective-permute-start.19) | collective-permute-done | bytes 81952 | tf_op jit(solution)/shard_map/ppermute | solution.py:356
  120.8 2.1 %collective-permute-done.18 = bf16[2,80,256]{2,1,0:T(8,128)(2,1)S(1)} collective-permute-done((bf16[2,80,256]{2,1,0:T(8,128)(2,1)S(1)}, bf16[2,80,256]{2,1,0:T(8,128)(2,1)S(1)}, u32[]{:S(2)}, u32[]{:S(2)}) %collective-permute-start.18) | collective-permute-done | bytes 81952 | tf_op jit(solution)/shard_map/ppermute | solution.py:356
  123.0 5.5 %collective-permute-start.21 = (bf16[4,2,80,256]{3,2,1,0:T(8,128)(2,1)S(1)}, bf16[4,2,80,256]{3,2,1,0:T(8,128)(2,1)S(1)}, u32[]{:S(2)}, u32[]{:S(2)}) collective-permute-start(bf16[4,2,80,256]{3,2,1,0:T(8,128)(2,1)S(1)} %pad_maximum_fusion.4.home_ref), channel_id=1, source_target_pairs={{0,8},{1,121},{2,10},{3,123},{4,12},{5,125},{6,14},{7,127},{8,16},... | collective-permute-start | bytes 983048 | tf_op jit(solution)/shard_map/ppermute | solution.py:356
  128.5 4.0 %collective-permute-done.21.near_ref = bf16[4,2,80,256]{3,2,1,0:T(8,128)(2,1)S(1)} collective-permute-done((bf16[4,2,80,256]{3,2,1,0:T(8,128)(2,1)S(1)}, bf16[4,2,80,256]{3,2,1,0:T(8,128)(2,1)S(1)}, u32[]{:S(2)}, u32[]{:S(2)}) %collective-permute-start.21) | collective-permute-done | bytes 327712 | tf_op jit(solution)/shard_map/ppermute | solution.py:356
  132.5 0.7 copy-done.8
  133.2 3.4 %shard_map.59.mat_ref = bf16[512,1024]{1,0:T(8,128)(2,1)} custom-call(s32[5]{0:T(128)} %stack.74.place_ref, s32[64,5]{1,0:T(8,128)} %copy.6.pattern_ref, bf16[4,2,80,256]{3,2,1,0:T(8,128)(2,1)} %copy-done.5, bf16[4,2,80,256]{3,2,1,0:T(8,128)(2,1)} %copy-done.8), custom_call_target="tpu_custom_call" | custom-call | tf_op jit(solution)/shard_map/pallas_call | solution.py:387
  136.7 5.7 %shard_map.61 = (bf16[4,8,32,256]{3,2,1,0:T(8,128)(2,1)}, bf16[4,8,32,256]{3,2,1,0:T(8,128)(2,1)}, bf16[4,8,32,256]{3,2,1,0:T(8,128)(2,1)}, bf16[4,8,32,256]{3,2,1,0:T(8,128)(2,1)}) custom-call(s32[5]{0:T(128)} %stack.74.place_ref, f32[256,128]{1,0:T(8,128)} %get-tuple-element.42.refs_6_.off_own_ref, f32[256,128]{1,0:T(8,128)} %get-tuple-element.45.refs_9_.off_near_ref, ...), custom_call_target="tpu_custom_call" | custom-call | tf_op jit(solution)/shard_map/pallas_call | solution.py:529
  142.5 4.1 %collective-permute-start.29 = (bf16[4,8,32,256]{3,2,1,0:T(8,128)(2,1)}, bf16[4,8,32,256]{3,2,1,0:T(8,128)(2,1)S(1)}, u32[]{:S(2)}, u32[]{:S(2)}) collective-permute-start(bf16[4,8,32,256]{3,2,1,0:T(8,128)(2,1)} %get-tuple-element.69), channel_id=1, source_target_pairs={{0,1},{1,0},{2,3},{3,2},{4,5},{5,4},{6,7},{7,6},{8,9},{9,8},{10,11... | collective-permute-start | bytes 1572872 | tf_op jit(solution)/shard_map/ppermute | solution.py:356
  146.6 5.8 %shard_map.60 = (bf16[4,8,32,256]{3,2,1,0:T(8,128)(2,1)}, bf16[4,8,32,256]{3,2,1,0:T(8,128)(2,1)}, bf16[4,8,32,256]{3,2,1,0:T(8,128)(2,1)}, bf16[4,8,32,256]{3,2,1,0:T(8,128)(2,1)}) custom-call(s32[5]{0:T(128)} %stack.74.place_ref, f32[256,128]{1,0:T(8,128)} %get-tuple-element.42.refs_6_.off_own_ref, f32[256,128]{1,0:T(8,128)} %get-tuple-element.45.refs_9_.off_near_ref, ...), custom_call_target="tpu_custom_call" | custom-call | tf_op jit(solution)/shard_map/pallas_call | solution.py:529
  152.5 3.2 %collective-permute-start.23 = (bf16[4,8,32,256]{3,2,1,0:T(8,128)(2,1)}, bf16[4,8,32,256]{3,2,1,0:T(8,128)(2,1)S(1)}, u32[]{:S(2)}, u32[]{:S(2)}) collective-permute-start(bf16[4,8,32,256]{3,2,1,0:T(8,128)(2,1)} %get-tuple-element.63), channel_id=1, source_target_pairs={{0,1},{1,0},{2,3},{3,2},{4,5},{5,4},{6,7},{7,6},{8,9},{9,8},{10,11... | collective-permute-start | bytes 1572872 | tf_op jit(solution)/shard_map/ppermute | solution.py:356
  155.8 0.2 add.57
  156.0 3.1 %collective-permute-done.30 = bf16[4,8,32,256]{3,2,1,0:T(8,128)(2,1)S(1)} collective-permute-done((bf16[4,8,32,256]{3,2,1,0:T(8,128)(2,1)}, bf16[4,8,32,256]{3,2,1,0:T(8,128)(2,1)S(1)}, u32[]{:S(2)}, u32[]{:S(2)}) %collective-permute-start.30) | collective-permute-done | bytes 524320 | tf_op jit(solution)/shard_map/ppermute | solution.py:356
  159.2 0.2 add.58
  159.6 1.8 collective-permute-start.32
  161.4 4.3 %collective-permute-done.22 = bf16[4,8,32,256]{3,2,1,0:T(8,128)(2,1)S(1)} collective-permute-done((bf16[4,8,32,256]{3,2,1,0:T(8,128)(2,1)}, bf16[4,8,32,256]{3,2,1,0:T(8,128)(2,1)S(1)}, u32[]{:S(2)}, u32[]{:S(2)}) %collective-permute-start.22) | collective-permute-done | bytes 524320 | tf_op jit(solution)/shard_map/ppermute | solution.py:356
  165.7 0.2 add.55
  166.0 4.5 %collective-permute-done.24 = bf16[4,8,32,256]{3,2,1,0:T(8,128)(2,1)S(1)} collective-permute-done((bf16[4,8,32,256]{3,2,1,0:T(8,128)(2,1)}, bf16[4,8,32,256]{3,2,1,0:T(8,128)(2,1)S(1)}, u32[]{:S(2)}, u32[]{:S(2)}) %collective-permute-start.24) | collective-permute-done | bytes 524320 | tf_op jit(solution)/shard_map/ppermute | solution.py:356
  170.4 0.2 add.56
  170.8 1.8 collective-permute-start.26
  172.7 1.0 collective-permute-start.27
  173.7 0.8 pad_maximum_fusion.5
  174.5 3.8 %collective-permute-done.25.rest_1_ = bf16[2,8,32,256]{3,2,1,0:T(8,128)(2,1)S(1)} collective-permute-done((bf16[2,8,32,256]{3,2,1,0:T(8,128)(2,1)S(1)}, bf16[2,8,32,256]{3,2,1,0:T(8,128)(2,1)S(1)}, u32[]{:S(2)}, u32[]{:S(2)}) %collective-permute-start.25) | collective-permute-done | bytes 262176 | tf_op jit(solution)/shard_map/ppermute | solution.py:356
  178.4 5.3 %collective-permute-done.26.rest_2_ = bf16[2,8,32,256]{3,2,1,0:T(8,128)(2,1)S(1)} collective-permute-done((bf16[2,8,32,256]{3,2,1,0:T(8,128)(2,1)S(1)}, bf16[2,8,32,256]{3,2,1,0:T(8,128)(2,1)S(1)}, u32[]{:S(2)}, u32[]{:S(2)}) %collective-permute-start.26) | collective-permute-done | bytes 262176 | tf_op jit(solution)/shard_map/ppermute | solution.py:356
  183.7 1.7 collective-permute-done.27.rest_3_
  185.5 0.7 copy-done.15
  186.2 4.3 %collect.1 = bf16[32,128,256]{2,1,0:T(8,128)(2,1)} custom-call(s32[32]{0:T(128)} %start_ref.3, s32[5]{0:T(128)} %stack.74.place_ref, bf16[2,8,32,256]{3,2,1,0:T(8,128)(2,1)} %get-tuple-element.103.rest_0_, bf16[2,8,32,256]{3,2,1,0:T(8,128)(2,1)} %copy-done.13, bf16[2,8,32,256]{3,2,1,0:T(8,128)(2,1)} %copy-done.14, bf16[2,8,32,256]{3,2,1,0:T(8,128)(2,1)} %copy-done.15, ...), custom_call_target="tpu_custom_call" | custom-call | tf_op jit(solution)/shard_map/collect/pallas_call | solution.py:545
  (81 shorter events, 1.2 us)
Async XLA Ops:
  0.0 61.5 %collective-permute-start = (f32[16,256]{1,0:T(8,128)}, f32[16,256]{1,0:T(8,128)S(1)}, u32[]{:S(2)}, u32[]{:S(2)}) collective-permute-start(f32[16,256]{1,0:T(8,128)} %param.8), channel_id=1, source_target_pairs={{0,121},{1,123},{2,125},{3,127},{4,0},{5,2},{6,4},{7,6},{8,1},{9,3... | collective-permute-start | bytes 49160 | tf_op jit(solution)/shard_map/ppermute | solution.py:384
  13.0 15.4 %collective-permute-start.7 = (bf16[2,8,32,256]{3,2,1,0:T(8,128)(2,1)}, bf16[2,8,32,256]{3,2,1,0:T(8,128)(2,1)S(1)}, u32[]{:S(2)}, u32[]{:S(2)}) collective-permute-start(bf16[2,8,32,256]{3,2,1,0:T(8,128)(2,1)} %get-tuple-element.47), channel_id=1, source_target_pairs={{0,2},{1,3},{2,4},{3,5},{4,6},{5,7},{6,0},{7,1},{8,10},{9,11},{10,... | collective-permute-start | bytes 786440 | tf_op jit(solution)/shard_map/ppermute | solution.py:356
  15.0 40.5 %collective-permute-start.8 = (bf16[2,8,32,256]{3,2,1,0:T(8,128)(2,1)}, bf16[2,8,32,256]{3,2,1,0:T(8,128)(2,1)S(1)}, u32[]{:S(2)}, u32[]{:S(2)}) collective-permute-start(bf16[2,8,32,256]{3,2,1,0:T(8,128)(2,1)} %get-tuple-element.48), channel_id=1, source_target_pairs={{0,4},{1,5},{2,6},{3,7},{4,0},{5,1},{6,2},{7,3},{8,12},{9,13},{10,... | collective-permute-start | bytes 786440 | tf_op jit(solution)/shard_map/ppermute | solution.py:356
  15.0 40.6 %collective-permute-start.9 = (bf16[2,8,32,256]{3,2,1,0:T(8,128)(2,1)}, bf16[2,8,32,256]{3,2,1,0:T(8,128)(2,1)S(1)}, u32[]{:S(2)}, u32[]{:S(2)}) collective-permute-start(bf16[2,8,32,256]{3,2,1,0:T(8,128)(2,1)} %get-tuple-element.49), channel_id=1, source_target_pairs={{0,6},{1,7},{2,0},{3,1},{4,2},{5,3},{6,4},{7,5},{8,14},{9,15},{10,... | collective-permute-start | bytes 786440 | tf_op jit(solution)/shard_map/ppermute | solution.py:356
  17.5 26.0 %collective-permute-start.1 = (bf16[2,11,32,256]{3,2,1,0:T(8,128)(2,1)}, bf16[2,11,32,256]{3,2,1,0:T(8,128)(2,1)S(1)}, u32[]{:S(2)}, u32[]{:S(2)}) collective-permute-start(bf16[2,11,32,256]{3,2,1,0:T(8,128)(2,1)} %get-tuple-element.39), channel_id=1, source_target_pairs={{0,2},{1,3},{2,4},{3,5},{4,6},{5,7},{6,0},{7,1},{8,10},{9,11},{10,... | collective-permute-start | bytes 1081352 | tf_op jit(solution)/shard_map/ppermute | solution.py:356
  28.4 15.2 %collective-permute-start.2 = (bf16[2,11,32,256]{3,2,1,0:T(8,128)(2,1)}, bf16[2,11,32,256]{3,2,1,0:T(8,128)(2,1)S(1)}, u32[]{:S(2)}, u32[]{:S(2)}) collective-permute-start(bf16[2,11,32,256]{3,2,1,0:T(8,128)(2,1)} %get-tuple-element.40), channel_id=1, source_target_pairs={{0,4},{1,5},{2,6},{3,7},{4,0},{5,1},{6,2},{7,3},{8,12},{9,13},{10,... | collective-permute-start | bytes 1081352 | tf_op jit(solution)/shard_map/ppermute | solution.py:356
  43.5 9.8 %collective-permute-start.3 = (bf16[2,11,32,256]{3,2,1,0:T(8,128)(2,1)}, bf16[2,11,32,256]{3,2,1,0:T(8,128)(2,1)S(1)}, u32[]{:S(2)}, u32[]{:S(2)}) collective-permute-start(bf16[2,11,32,256]{3,2,1,0:T(8,128)(2,1)} %get-tuple-element.41), channel_id=1, source_target_pairs={{0,6},{1,7},{2,0},{3,1},{4,2},{5,3},{6,4},{7,5},{8,14},{9,15},{10,... | collective-permute-start | bytes 1081352 | tf_op jit(solution)/shard_map/ppermute | solution.py:356
  54.3 7.7 %collective-permute-start.4 = (bf16[4,11,32,256]{3,2,1,0:T(8,128)(2,1)}, bf16[4,11,32,256]{3,2,1,0:T(8,128)(2,1)S(1)}, u32[]{:S(2)}, u32[]{:S(2)}) collective-permute-start(bf16[4,11,32,256]{3,2,1,0:T(8,128)(2,1)} %pad_maximum_fusion.1), channel_id=1, source_target_pairs={{0,1},{1,0},{2,3},{3,2},{4,5},{5,4},{6,7},{7,6},{8,9},{9,8},{10,11... | collective-permute-start | bytes 2162696 | tf_op jit(solution)/shard_map/ppermute | solution.py:356
  55.6 6.4 %copy-start.16 = (s32[64,5]{0,1:T(8,128)S(1)}, s32[64,5]{0,1:T(8,128)}, u32[]{:S(2)}) copy-start(s32[64,5]{0,1:T(8,128)} %param.9) | copy-start | bytes 3844
  55.6 20.9 %collective-permute-start.6 = (bf16[4,11,32,256]{3,2,1,0:T(8,128)(2,1)}, bf16[4,11,32,256]{3,2,1,0:T(8,128)(2,1)S(1)}, u32[]{:S(2)}, u32[]{:S(2)}) collective-permute-start(bf16[4,11,32,256]{3,2,1,0:T(8,128)(2,1)} %pad_maximum_fusion.1), channel_id=1, source_target_pairs={{0,121},{1,8},{2,123},{3,10},{4,125},{5,12},{6,127},{7,14},{8,1},{... | collective-permute-start | bytes 2162696 | tf_op jit(solution)/shard_map/ppermute | solution.py:356
  55.8 7.0 %copy-start = (bf16[4,11,32,256]{3,2,1,0:T(8,128)(2,1)}, bf16[4,11,32,256]{3,2,1,0:T(8,128)(2,1)S(1)}, u32[]{:S(2)}) copy-start(bf16[4,11,32,256]{3,2,1,0:T(8,128)(2,1)S(1)} %pad_maximum_fusion.refs_0_.refs_2_.refs_3_) | copy-start | bytes 2162692
  55.8 20.7 %collective-permute-start.5 = (bf16[4,11,32,256]{3,2,1,0:T(8,128)(2,1)S(1)}, bf16[4,11,32,256]{3,2,1,0:T(8,128)(2,1)S(1)}, u32[]{:S(2)}, u32[]{:S(2)}) collective-permute-start(bf16[4,11,32,256]{3,2,1,0:T(8,128)(2,1)S(1)} %pad_maximum_fusion.refs_0_.refs_2_.refs_3_), channel_id=1, source_target_pairs={{0,8},{1,121},{2,10},{3,123},{4,12},{5,125},{6,14},{7,127},{8,16},... | collective-permute-start | bytes 2162696 | tf_op jit(solution)/shard_map/ppermute | solution.py:356
  61.4 6.6 %collective-permute-start.12 = (bf16[4,8,32,256]{3,2,1,0:T(8,128)(2,1)}, bf16[4,8,32,256]{3,2,1,0:T(8,128)(2,1)}, u32[]{:S(2)}, u32[]{:S(2)}) collective-permute-start(bf16[4,8,32,256]{3,2,1,0:T(8,128)(2,1)} %pad_maximum_fusion.3), channel_id=1, source_target_pairs={{0,1},{1,0},{2,3},{3,2},{4,5},{5,4},{6,7},{7,6},{8,9},{9,8},{10,11... | collective-permute-start | bytes 1572872 | tf_op jit(solution)/shard_map/ppermute | solution.py:356
  61.5 6.6 %copy-start.4 = (bf16[4,8,32,256]{3,2,1,0:T(8,128)(2,1)}, bf16[4,8,32,256]{3,2,1,0:T(8,128)(2,1)S(1)}, u32[]{:S(2)}) copy-start(bf16[4,8,32,256]{3,2,1,0:T(8,128)(2,1)S(1)} %pad_maximum_fusion.2.refs_0_) | copy-start | bytes 1572868
  61.5 1.3 copy-start.9
  61.5 23.3 %collective-permute-start.10 = (bf16[4,8,32,256]{3,2,1,0:T(8,128)(2,1)S(1)}, bf16[4,8,32,256]{3,2,1,0:T(8,128)(2,1)}, u32[]{:S(2)}, u32[]{:S(2)}) collective-permute-start(bf16[4,8,32,256]{3,2,1,0:T(8,128)(2,1)S(1)} %pad_maximum_fusion.2.refs_0_), channel_id=1, source_target_pairs={{0,8},{1,121},{2,10},{3,123},{4,12},{5,125},{6,14},{7,127},{8,16},... | collective-permute-start | bytes 1572872 | tf_op jit(solution)/shard_map/ppermute | solution.py:356
  62.0 0.9 copy-start.1
  62.0 23.4 %collective-permute-start.11 = (bf16[4,8,32,256]{3,2,1,0:T(8,128)(2,1)}, bf16[4,8,32,256]{3,2,1,0:T(8,128)(2,1)}, u32[]{:S(2)}, u32[]{:S(2)}) collective-permute-start(bf16[4,8,32,256]{3,2,1,0:T(8,128)(2,1)} %pad_maximum_fusion.3), channel_id=1, source_target_pairs={{0,121},{1,8},{2,123},{3,10},{4,125},{5,12},{6,127},{7,14},{8,1},{... | collective-permute-start | bytes 1572872 | tf_op jit(solution)/shard_map/ppermute | solution.py:356
  76.5 0.9 copy-start.3
  76.5 1.1 copy-start.2
  93.9 7.3 %collective-permute-start.13 = (bf16[2,80,512]{2,1,0:T(8,128)(2,1)}, bf16[2,80,512]{2,1,0:T(8,128)(2,1)S(1)}, u32[]{:S(2)}, u32[]{:S(2)}) collective-permute-start(bf16[2,80,512]{2,1,0:T(8,128)(2,1)} %get-tuple-element.56), channel_id=1, source_target_pairs={{0,2},{1,3},{2,4},{3,5},{4,6},{5,7},{6,0},{7,1},{8,10},{9,11},{10,... | collective-permute-start | bytes 491528 | tf_op jit(solution)/shard_map/ppermute | solution.py:356
  93.9 7.3 %collective-permute-start.14 = (bf16[2,80,512]{2,1,0:T(8,128)(2,1)}, bf16[2,80,512]{2,1,0:T(8,128)(2,1)S(1)}, u32[]{:S(2)}, u32[]{:S(2)}) collective-permute-start(bf16[2,80,512]{2,1,0:T(8,128)(2,1)} %get-tuple-element.57), channel_id=1, source_target_pairs={{0,4},{1,5},{2,6},{3,7},{4,0},{5,1},{6,2},{7,3},{8,12},{9,13},{10,... | collective-permute-start | bytes 491528 | tf_op jit(solution)/shard_map/ppermute | solution.py:356
  96.3 5.9 %collective-permute-start.15 = (bf16[2,80,512]{2,1,0:T(8,128)(2,1)}, bf16[2,80,512]{2,1,0:T(8,128)(2,1)S(1)}, u32[]{:S(2)}, u32[]{:S(2)}) collective-permute-start(bf16[2,80,512]{2,1,0:T(8,128)(2,1)} %get-tuple-element.58), channel_id=1, source_target_pairs={{0,6},{1,7},{2,0},{3,1},{4,2},{5,3},{6,4},{7,5},{8,14},{9,15},{10,... | collective-permute-start | bytes 491528 | tf_op jit(solution)/shard_map/ppermute | solution.py:356
  103.2 8.6 %collective-permute-start.16 = (bf16[2,80,256]{2,1,0:T(8,128)(2,1)S(1)}, bf16[2,80,256]{2,1,0:T(8,128)(2,1)S(1)}, u32[]{:S(2)}, u32[]{:S(2)}) collective-permute-start(bf16[2,80,256]{2,1,0:T(8,128)(2,1)S(1)} %slice.169), channel_id=1, source_target_pairs={{0,120},{1,9},{2,122},{3,11},{4,124},{5,13},{6,126},{7,15},{8,0},{... | collective-permute-start | bytes 245768 | tf_op jit(solution)/shard_map/ppermute | solution.py:356
  111.8 1.7 collective-permute-start.17
  113.6 4.1 %collective-permute-start.20 = (bf16[2,80,256]{2,1,0:T(8,128)(2,1)S(1)}, bf16[2,80,256]{2,1,0:T(8,128)(2,1)S(1)}, u32[]{:S(2)}, u32[]{:S(2)}) collective-permute-start(bf16[2,80,256]{2,1,0:T(8,128)(2,1)S(1)} %add_convert_fusion), channel_id=1, source_target_pairs={{0,6},{1,7},{2,0},{3,1},{4,2},{5,3},{6,4},{7,5},{8,14},{9,15},{10,... | collective-permute-start | bytes 245768 | tf_op jit(solution)/shard_map/ppermute | solution.py:356
  115.9 4.9 %collective-permute-start.19 = (bf16[2,80,256]{2,1,0:T(8,128)(2,1)S(1)}, bf16[2,80,256]{2,1,0:T(8,128)(2,1)S(1)}, u32[]{:S(2)}, u32[]{:S(2)}) collective-permute-start(bf16[2,80,256]{2,1,0:T(8,128)(2,1)S(1)} %add_convert_fusion), channel_id=1, source_target_pairs={{0,4},{1,5},{2,6},{3,7},{4,0},{5,1},{6,2},{7,3},{8,12},{9,13},{10,... | collective-permute-start | bytes 245768 | tf_op jit(solution)/shard_map/ppermute | solution.py:356
  115.9 7.0 %collective-permute-start.18 = (bf16[2,80,256]{2,1,0:T(8,128)(2,1)S(1)}, bf16[2,80,256]{2,1,0:T(8,128)(2,1)S(1)}, u32[]{:S(2)}, u32[]{:S(2)}) collective-permute-start(bf16[2,80,256]{2,1,0:T(8,128)(2,1)S(1)} %add_convert_fusion), channel_id=1, source_target_pairs={{0,2},{1,3},{2,4},{3,5},{4,6},{5,7},{6,0},{7,1},{8,10},{9,11},{10,... | collective-permute-start | bytes 245768 | tf_op jit(solution)/shard_map/ppermute | solution.py:356
  123.0 9.5 %copy-start.5 = (bf16[4,2,80,256]{3,2,1,0:T(8,128)(2,1)}, bf16[4,2,80,256]{3,2,1,0:T(8,128)(2,1)S(1)}, u32[]{:S(2)}) copy-start(bf16[4,2,80,256]{3,2,1,0:T(8,128)(2,1)S(1)} %pad_maximum_fusion.4.home_ref) | copy-start | bytes 983044
  123.0 9.5 %collective-permute-start.21 = (bf16[4,2,80,256]{3,2,1,0:T(8,128)(2,1)S(1)}, bf16[4,2,80,256]{3,2,1,0:T(8,128)(2,1)S(1)}, u32[]{:S(2)}, u32[]{:S(2)}) collective-permute-start(bf16[4,2,80,256]{3,2,1,0:T(8,128)(2,1)S(1)} %pad_maximum_fusion.4.home_ref), channel_id=1, source_target_pairs={{0,8},{1,121},{2,10},{3,123},{4,12},{5,125},{6,14},{7,127},{8,16},... | collective-permute-start | bytes 983048 | tf_op jit(solution)/shard_map/ppermute | solution.py:356
  132.5 0.7 copy-start.8
  142.4 13.3 %collective-permute-start.28 = (bf16[4,8,32,256]{3,2,1,0:T(8,128)(2,1)}, bf16[4,8,32,256]{3,2,1,0:T(8,128)(2,1)S(1)}, u32[]{:S(2)}, u32[]{:S(2)}) collective-permute-start(bf16[4,8,32,256]{3,2,1,0:T(8,128)(2,1)} %get-tuple-element.68), channel_id=1, source_target_pairs={{0,120},{1,9},{2,122},{3,11},{4,124},{5,13},{6,126},{7,15},{8,0},{... | collective-permute-start | bytes 1572872 | tf_op jit(solution)/shard_map/ppermute | solution.py:356
  142.5 13.5 %collective-permute-start.29 = (bf16[4,8,32,256]{3,2,1,0:T(8,128)(2,1)}, bf16[4,8,32,256]{3,2,1,0:T(8,128)(2,1)S(1)}, u32[]{:S(2)}, u32[]{:S(2)}) collective-permute-start(bf16[4,8,32,256]{3,2,1,0:T(8,128)(2,1)} %get-tuple-element.69), channel_id=1, source_target_pairs={{0,1},{1,0},{2,3},{3,2},{4,5},{5,4},{6,7},{7,6},{8,9},{9,8},{10,11... | collective-permute-start | bytes 1572872 | tf_op jit(solution)/shard_map/ppermute | solution.py:356
  146.6 12.6 %collective-permute-start.30 = (bf16[4,8,32,256]{3,2,1,0:T(8,128)(2,1)}, bf16[4,8,32,256]{3,2,1,0:T(8,128)(2,1)S(1)}, u32[]{:S(2)}, u32[]{:S(2)}) collective-permute-start(bf16[4,8,32,256]{3,2,1,0:T(8,128)(2,1)} %get-tuple-element.70), channel_id=1, source_target_pairs={{0,121},{1,8},{2,123},{3,10},{4,125},{5,12},{6,127},{7,14},{8,1},{... | collective-permute-start | bytes 1572872 | tf_op jit(solution)/shard_map/ppermute | solution.py:356
  146.6 9.2 %copy-start.7 = (bf16[4,8,32,256]{3,2,1,0:T(8,128)(2,1)S(1)}, bf16[4,8,32,256]{3,2,1,0:T(8,128)(2,1)}, u32[]{:S(2)}) copy-start(bf16[4,8,32,256]{3,2,1,0:T(8,128)(2,1)} %get-tuple-element.67) | copy-start | bytes 1572868
  152.4 13.3 %collective-permute-start.22 = (bf16[4,8,32,256]{3,2,1,0:T(8,128)(2,1)}, bf16[4,8,32,256]{3,2,1,0:T(8,128)(2,1)S(1)}, u32[]{:S(2)}, u32[]{:S(2)}) collective-permute-start(bf16[4,8,32,256]{3,2,1,0:T(8,128)(2,1)} %get-tuple-element.62), channel_id=1, source_target_pairs={{0,120},{1,9},{2,122},{3,11},{4,124},{5,13},{6,126},{7,15},{8,0},{... | collective-permute-start | bytes 1572872 | tf_op jit(solution)/shard_map/ppermute | solution.py:356
  152.5 13.5 %collective-permute-start.23 = (bf16[4,8,32,256]{3,2,1,0:T(8,128)(2,1)}, bf16[4,8,32,256]{3,2,1,0:T(8,128)(2,1)S(1)}, u32[]{:S(2)}, u32[]{:S(2)}) collective-permute-start(bf16[4,8,32,256]{3,2,1,0:T(8,128)(2,1)} %get-tuple-element.63), channel_id=1, source_target_pairs={{0,1},{1,0},{2,3},{3,2},{4,5},{5,4},{6,7},{7,6},{8,9},{9,8},{10,11... | collective-permute-start | bytes 1572872 | tf_op jit(solution)/shard_map/ppermute | solution.py:356
  155.7 14.7 %collective-permute-start.24 = (bf16[4,8,32,256]{3,2,1,0:T(8,128)(2,1)}, bf16[4,8,32,256]{3,2,1,0:T(8,128)(2,1)S(1)}, u32[]{:S(2)}, u32[]{:S(2)}) collective-permute-start(bf16[4,8,32,256]{3,2,1,0:T(8,128)(2,1)} %get-tuple-element.64), channel_id=1, source_target_pairs={{0,121},{1,8},{2,123},{3,10},{4,125},{5,12},{6,127},{7,14},{8,1},{... | collective-permute-start | bytes 1572872 | tf_op jit(solution)/shard_map/ppermute | solution.py:356
  156.0 9.7 %copy-start.6 = (bf16[4,8,32,256]{3,2,1,0:T(8,128)(2,1)S(1)}, bf16[4,8,32,256]{3,2,1,0:T(8,128)(2,1)}, u32[]{:S(2)}) copy-start(bf16[4,8,32,256]{3,2,1,0:T(8,128)(2,1)} %get-tuple-element.61) | copy-start | bytes 1572868
  159.4 13.2 %collective-permute-start.31 = (bf16[2,8,32,256]{3,2,1,0:T(8,128)(2,1)S(1)}, bf16[2,8,32,256]{3,2,1,0:T(8,128)(2,1)S(1)}, u32[]{:S(2)}, u32[]{:S(2)}) collective-permute-start(bf16[2,8,32,256]{3,2,1,0:T(8,128)(2,1)S(1)} %pad_maximum_fusion.10), channel_id=1, source_target_pairs={{0,2},{1,3},{2,4},{3,5},{4,6},{5,7},{6,0},{7,1},{8,10},{9,11},{10,... | collective-permute-start | bytes 786440 | tf_op jit(solution)/shard_map/ppermute | solution.py:356
  159.6 15.0 %collective-permute-start.32 = (bf16[2,8,32,256]{3,2,1,0:T(8,128)(2,1)S(1)}, bf16[2,8,32,256]{3,2,1,0:T(8,128)(2,1)S(1)}, u32[]{:S(2)}, u32[]{:S(2)}) collective-permute-start(bf16[2,8,32,256]{3,2,1,0:T(8,128)(2,1)S(1)} %pad_maximum_fusion.11), channel_id=1, source_target_pairs={{0,4},{1,5},{2,6},{3,7},{4,0},{5,1},{6,2},{7,3},{8,12},{9,13},{10,... | collective-permute-start | bytes 786440 | tf_op jit(solution)/shard_map/ppermute | solution.py:356
  165.7 8.8 %collective-permute-start.33 = (bf16[2,8,32,256]{3,2,1,0:T(8,128)(2,1)S(1)}, bf16[2,8,32,256]{3,2,1,0:T(8,128)(2,1)S(1)}, u32[]{:S(2)}, u32[]{:S(2)}) collective-permute-start(bf16[2,8,32,256]{3,2,1,0:T(8,128)(2,1)S(1)} %pad_maximum_fusion.12), channel_id=1, source_target_pairs={{0,6},{1,7},{2,0},{3,1},{4,2},{5,3},{6,4},{7,5},{8,14},{9,15},{10,... | collective-permute-start | bytes 786440 | tf_op jit(solution)/shard_map/ppermute | solution.py:356
  170.7 7.7 %collective-permute-start.25 = (bf16[2,8,32,256]{3,2,1,0:T(8,128)(2,1)S(1)}, bf16[2,8,32,256]{3,2,1,0:T(8,128)(2,1)S(1)}, u32[]{:S(2)}, u32[]{:S(2)}) collective-permute-start(bf16[2,8,32,256]{3,2,1,0:T(8,128)(2,1)S(1)} %pad_maximum_fusion.6), channel_id=1, source_target_pairs={{0,2},{1,3},{2,4},{3,5},{4,6},{5,7},{6,0},{7,1},{8,10},{9,11},{10,... | collective-permute-start | bytes 786440 | tf_op jit(solution)/shard_map/ppermute | solution.py:356
  170.8 12.9 %collective-permute-start.26 = (bf16[2,8,32,256]{3,2,1,0:T(8,128)(2,1)S(1)}, bf16[2,8,32,256]{3,2,1,0:T(8,128)(2,1)S(1)}, u32[]{:S(2)}, u32[]{:S(2)}) collective-permute-start(bf16[2,8,32,256]{3,2,1,0:T(8,128)(2,1)S(1)} %pad_maximum_fusion.7), channel_id=1, source_target_pairs={{0,4},{1,5},{2,6},{3,7},{4,0},{5,1},{6,2},{7,3},{8,12},{9,13},{10,... | collective-permute-start | bytes 786440 | tf_op jit(solution)/shard_map/ppermute | solution.py:356
  172.7 12.8 %copy-start.10 = (bf16[2,8,32,256]{3,2,1,0:T(8,128)(2,1)}, bf16[2,8,32,256]{3,2,1,0:T(8,128)(2,1)S(1)}, u32[]{:S(2)}) copy-start(bf16[2,8,32,256]{3,2,1,0:T(8,128)(2,1)S(1)} %collective-permute-done.31.rest_5_) | copy-start | bytes 786436
  172.7 12.8 %collective-permute-start.27 = (bf16[2,8,32,256]{3,2,1,0:T(8,128)(2,1)S(1)}, bf16[2,8,32,256]{3,2,1,0:T(8,128)(2,1)S(1)}, u32[]{:S(2)}, u32[]{:S(2)}) collective-permute-start(bf16[2,8,32,256]{3,2,1,0:T(8,128)(2,1)S(1)} %pad_maximum_fusion.8), channel_id=1, source_target_pairs={{0,6},{1,7},{2,0},{3,1},{4,2},{5,3},{6,4},{7,5},{8,14},{9,15},{10,... | collective-permute-start | bytes 786440 | tf_op jit(solution)/shard_map/ppermute | solution.py:356
  174.5 11.0 %copy-start.11 = (bf16[2,8,32,256]{3,2,1,0:T(8,128)(2,1)}, bf16[2,8,32,256]{3,2,1,0:T(8,128)(2,1)S(1)}, u32[]{:S(2)}) copy-start(bf16[2,8,32,256]{3,2,1,0:T(8,128)(2,1)S(1)} %collective-permute-done.32.rest_6_) | copy-start | bytes 786436
  174.5 11.0 %copy-start.12 = (bf16[2,8,32,256]{3,2,1,0:T(8,128)(2,1)}, bf16[2,8,32,256]{3,2,1,0:T(8,128)(2,1)S(1)}, u32[]{:S(2)}) copy-start(bf16[2,8,32,256]{3,2,1,0:T(8,128)(2,1)S(1)} %collective-permute-done.33.rest_7_) | copy-start | bytes 786436
  178.4 7.1 %copy-start.13 = (bf16[2,8,32,256]{3,2,1,0:T(8,128)(2,1)}, bf16[2,8,32,256]{3,2,1,0:T(8,128)(2,1)S(1)}, u32[]{:S(2)}) copy-start(bf16[2,8,32,256]{3,2,1,0:T(8,128)(2,1)S(1)} %collective-permute-done.25.rest_1_) | copy-start | bytes 786436
  183.7 1.8 copy-start.14
  185.5 0.7 copy-start.15
where the time goes:
time: 191 us
  waiting for transfers between devices  86.1 us (45%)
  Pallas kernels  49.8 us (26%)
  starting transfers between devices  43.1 us (23%)
  local copies, waits for them, and re-layouts  6.33 us (3%)
  other arithmetic  4.76 us (2%)
    ppermute x33, waiting for transfers between devices, send(): return lax.ppermute(array, axes, pairs)  86.1 us
    ppermute x33, starting transfers between devices, send(): return lax.ppermute(array, axes, pairs)  35.3 us
    pallas_call x5, Pallas kernels, call(): pl.pallas_call(kernel, grid=(1,), out_shape=outs, in_specs=[smem()] * sme...  29.3 us
    pallas_call x2, Pallas kernels, body(): pl.pallas_call(functools.partial(gradient_kernel, start=cuts[which], scal...  11.6 us
    ppermute x1, starting transfers between devices, body(): window_pot = lax.ppermute(potential, axes, pot_pairs)  7.78 us
    pallas_call x1, Pallas kernels, body(): pl.pallas_call(functools.partial(spread_kernel, cuts=cuts), grid=(2,), ou...  4.58 us
    pallas_call x1, Pallas kernels, body(): pl.pallas_call(functools.partial(collect_kernel, cuts=cuts), grid=(2,), o...  4.33 us
  transfers between devices with their start and end apart: 34, of which 20 were waited for; matrix products, arithmetic and copies ran while one was open for 4% of the time, Pallas kernels for 15%

commit v1 on v0

--- a/solution.py
+++ b/solution.py
@@ -15,26 +15,45 @@
 
 
 def params():
-    return pltpu.CompilerParams(vmem_limit_bytes=56 * 1024 * 1024)
+    return pltpu.CompilerParams(vmem_limit_bytes=24 * 1024 * 1024)
 
 
 def smem():
     return pl.BlockSpec(memory_space=pltpu.SMEM)
 
 
-def fixed(*shape):
-    return pl.BlockSpec(shape, lambda t: (0,) * len(shape))
+def vmem():
+    return pl.BlockSpec(memory_space=pltpu.VMEM)
+
+
+def near_core(array):
+    return pltpu.with_memory_space_constraint(array, pltpu.VMEM)
 
 
 def shaped(shape, dtype=BF16):
-    return jax.ShapeDtypeStruct(shape, dtype)
+    return pltpu.VMEM(shape, dtype)
+
+
+class Place:
+    def __init__(self):
+        slab = lax.axis_index("slab").astype(jnp.int32)
+        orb = lax.axis_index("orb").astype(jnp.int32)
+        slabs, levels = lax.axis_size("slab"), lax.axis_size("orb") // 2
+        core, level = orb & 1, orb // 2
+        near = lax.rem(slab + slabs - 1 + 2 * core, jnp.int32(slabs))
+        position = (core * levels + level) * 16 + 64
+        self.items = [position, slab, near, level, core]
+
+    def __getitem__(self, at):
+        return self.items[at]
 
 
 def other_core(place_ref, side):
     return place_ref[4] if side == 0 else 1 - place_ref[4]
 
 
-def spread_kernel(start_ref, place_ref, x_ref, *rest, cuts):
+def spread_kernel(start_ref, x_ref, *rest, cuts):
+    place_ref = Place()
     outs, scratch = rest[:-1], rest[-1]
     held, length, cross = x_ref.shape
     levels = 4
@@ -44,6 +63,7 @@
         lax.broadcasted_iota(jnp.int32, (length, length), 0)
         - lax.broadcasted_iota(jnp.int32, (length, length), 1)
     ) & (length - 1)
+    mine = pl.ds(pl.multiple_of(pl.program_id(0) * held, held), held)
     which_row = lax.broadcasted_iota(jnp.int32, (held, cross), 0)
     offsets = jnp.zeros((held, cross), jnp.int32)
     for j in range(held):
@@ -58,13 +78,13 @@
     for d in range(levels):
         for side in range(2):
             group = other_core(place_ref, side) * levels + ((place_ref[3] + d) & (levels - 1))
-            outs[d][side, 0] = offsets
+            outs[d][side, 0, mine, :] = offsets
             for which, (first, last) in enumerate(spans(cuts)):
                 for q in range(first, last):
                     row = (group * narrow + q - 1) & (length - 1)
                     to = q - first + (1 if which == 0 else 0)
                     for half in range(cross // 128):
-                        outs[which * levels + d][side, to, :, half * 128 : half * 128 + 128] = scratch[
+                        outs[which * levels + d][side, to, mine, half * 128 : half * 128 + 128] = scratch[
                             half, pl.ds(pl.multiple_of(row * held, held), held), :
                         ].astype(BF16)
 
@@ -75,7 +95,8 @@
     ]
 
 
-def collect_kernel(start_ref, place_ref, *rest, cuts):
+def collect_kernel(start_ref, *rest, cuts):
+    place_ref = Place()
     levels = 4
     out_ref, scratch = rest[-2], rest[-1]
     held, length, cross = out_ref.shape
@@ -85,6 +106,7 @@
         lax.broadcasted_iota(jnp.int32, (length, length), 1)
         - lax.broadcasted_iota(jnp.int32, (length, length), 0)
     ) & (length - 1)
+    mine = pl.ds(pl.multiple_of(pl.program_id(0) * held, held), held)
     for which in range(len(cuts) - 1):
         wide = 4 * (cuts[which + 1] - cuts[which])
         for d in range(levels):
@@ -93,7 +115,7 @@
                 first = (group * narrow + 4 * cuts[which]) * held
                 for half in range(cross // 128):
                     scratch[half, pl.ds(pl.multiple_of(first, 4 * held), wide * held), :] = (
-                        rest[which * levels + d][side, :, :, half * 128 : half * 128 + 128]
+                        rest[which * levels + d][side, :, mine, half * 128 : half * 128 + 128]
                         .reshape(wide * held, 128)
                         .astype(F32)
                     )
@@ -122,27 +144,28 @@
         lanes = slice((col % 4) * cross, (col % 4 + 1) * cross)
         now = start * 4 + col
         for (d, side), at in zip(units, places):
-            place = place_ref[0] + now - off_ref[pl.ds(at, held), :].astype(jnp.int32)
-            inside = (place >= 0) & (place < 128)
+            place = place_ref[0] + now - off_ref[pl.ds(at, held), :]
+            inside = (place & -128) == 0
             keep = jnp.where(inside, 1.0, 0.0) if own else jnp.where(inside, 0.0, 1.0)
+            keep = keep.astype(BF16)
             keep = jnp.concatenate([keep, keep], axis=1)
-            phi_ref[col // 4, pl.ds(at, held), lanes] = (
-                row_at(side, d, now + 1).astype(F32) * keep
-            ).astype(BF16)
+            phi_ref[col // 4, pl.ds(at, held), lanes] = row_at(side, d, now + 1) * keep
         across_ref[...] = jnp.dot(
             phi_ref[col // 4, :, lanes], kin_ref[...], preferred_element_type=F32
         )
         for (d, side), at in zip(units, places):
-            place = place_ref[0] + now - off_ref[pl.ds(at, held), :].astype(jnp.int32)
-            inside = (place >= 0) & (place < 128)
+            place = place_ref[0] + now - off_ref[pl.ds(at, held), :]
+            inside = (place & -128) == 0
             keep = jnp.where(inside, 0.5, 0.0) if own else jnp.where(inside, 0.0, 0.5)
             row = place & 127
-            left = jnp.where(row == 0, 0.0, keep)
-            right = jnp.where(row == 127, 0.0, keep)
+            left = jnp.where(row == 0, 0.0, keep).astype(BF16)
+            right = jnp.where(row == 127, 0.0, keep).astype(BF16)
             left = jnp.concatenate([left, left], axis=1)
             right = jnp.concatenate([right, right], axis=1)
             phi = phi_ref[col // 4, pl.ds(at, held), lanes].astype(F32)
-            around = row_at(side, d, now).astype(F32) * left + row_at(side, d, now + 2).astype(F32) * right
+            around = (row_at(side, d, now) * left).astype(F32) + (
+                row_at(side, d, now + 2) * right
+            ).astype(F32)
             kin = (phi - around + across_ref[pl.ds(at, held), :]).astype(BF16).astype(F32)
             app_ref[col // 4, pl.ds(at, held), lanes] = (
                 kin + pot_ref[now : now + 1, :] * phi
@@ -157,18 +180,19 @@
             return pair[side][d, q + 1]
 
         return row_at, rest
-    pair, edges, rest = refs[:2], refs[2:6], refs[6:]
+    pair, edges, rest = refs[:2], refs[2:4], refs[4:]
     first = spans(cuts)[which][0]
 
     def row_at(side, d, q):
         if q >= first:
             return pair[side][d, q - first]
-        return edges[2 * side + q - first + 2][d, 0]
+        return edges[side][d, edges[side].shape[1] + q - first]
 
     return row_at, rest
 
 
-def own_kernel(place_ref, pot_ref, kin_ref, *refs, which, cuts):
+def own_kernel(pot_ref, kin_ref, *refs, which, cuts):
+    place_ref = Place()
     row_at, rest = chunk_inputs(refs, which, cuts)
     if which == 0:
         phi_ref, app_ref, pair_ref, off_ref, across_ref = rest
@@ -196,10 +220,13 @@
     for side in range(2):
         for d in range(levels):
             unit = ((place_ref[3] - d) & (levels - 1)) * 2 + other_core(place_ref, side)
-            off_ref[pl.ds(pl.multiple_of(unit * held, held), held), :] = refs[side][d, 0][:, :128].astype(F32)
-
-
-def near_kernel(place_ref, pattern_ref, pot_ref, kin_ref, *refs, which, cuts, scale):
+            off_ref[pl.ds(pl.multiple_of(unit * held, held), held), :] = (
+                refs[side][d, 0][:, :128].astype(F32).astype(jnp.int32)
+            )
+
+
+def near_kernel(pattern_ref, pot_ref, kin_ref, *refs, which, cuts, scale):
+    place_ref = Place()
     row_at, rest = chunk_inputs(refs, which, cuts)
     last = which == len(cuts) - 2
     phi_own_ref, app_own_ref, rest = rest[0], rest[1], rest[2:]
@@ -266,18 +293,20 @@
 def local_block(place_ref, pattern_ref, block, slot, per_slab):
     home, near = place_ref[1], place_ref[2]
     base = home if block < per_slab else near
-    listed = pattern_ref[base * per_slab + block % per_slab, slot]
+    listed = pattern_ref[slot, base * per_slab + block % per_slab]
     slab = listed // per_slab
     inner = listed % per_slab
     return jnp.where(slab == home, inner, jnp.where(slab == near, per_slab + inner, 2 * per_slab))
 
 
-def unpack_kernel(place_ref, pattern_ref, home_ref, near_ref, out_ref):
+def unpack_kernel(pattern_ref, *rest):
+    place_ref = Place()
+    out_ref = rest[8]
     total = out_ref.shape[0]
     per_slab = total // 2 // BLOCK
     low = lax.broadcasted_iota(jnp.int32, (16, 128), 1) < BLOCK
     for group in range(total // 128):
-        parts = home_ref if group < total // 256 else near_ref
+        parts = rest[:4] if group < total // 256 else rest[4:8]
         first = group * 128 % (total // 2)
         lanes = slice(first, first + 128)
         found = []
@@ -288,26 +317,30 @@
             ]
             found.append(jnp.where(low, first, second))
         for block in range(2 * per_slab):
-            hits = [jnp.where(found[slot] == block, 1.0, 0.0) for slot in range(5)]
+            hits = [
+                jnp.where(found[slot] == block, 1.0, 0.0).astype(BF16) for slot in range(5)
+            ]
             for by in range(4):
                 quarter = (place_ref[3] - by) & 3
                 side = (quarter // 2) ^ place_ref[4]
                 d = (block % per_slab - place_ref[3]) & 3
                 row = ((block // per_slab * 2 + side) * 4 + d) * 32 + (quarter % 2) * 16
                 for kind in range(2):
-                    acc = jnp.zeros((16, 128), F32)
-                    for slot in range(5):
-                        part = parts[by, kind, slot * 16 : slot * 16 + 16, lanes].astype(F32)
-                        acc = acc + part * hits[slot]
+                    terms = [
+                        parts[by][kind, slot * 16 : slot * 16 + 16, lanes] * hits[slot]
+                        for slot in range(5)
+                    ]
+                    acc = (terms[0] + terms[1]) + (terms[2] + terms[3]) + terms[4]
                     if kind == 1:
                         acc = -acc
                     out_ref[
                         pl.ds(pl.multiple_of(row, 16), 16),
                         kind * total + group * 128 : kind * total + group * 128 + 128,
-                    ] = acc.astype(BF16)
-
-
-def gradient_kernel(place_ref, off_own_ref, off_near_ref, mat_ref, *rest, start, scale):
+                    ] = acc
+
+
+def gradient_kernel(off_own_ref, off_near_ref, mat_ref, *rest, start, scale):
+    place_ref = Place()
     ins, outs = rest[:4], rest[4:]
     levels, _, held, cross = outs[0].shape
     phi_own_ref, app_own_ref, phi_ref, app_ref = ins
@@ -317,29 +350,28 @@
             for d in range(levels):
                 unit = ((place_ref[3] + d) & (levels - 1)) * 2 + other_core(place_ref, side)
                 seats.append(
-                    ref[pl.ds(pl.multiple_of(unit * held, held), held), :].astype(jnp.int32)
+                    ref[pl.ds(pl.multiple_of(unit * held, held), held), :]
                 )
-    right = jnp.concatenate([app_own_ref[0], app_ref[0], phi_own_ref[0], phi_ref[0]], axis=0)
+    quad = pl.program_id(0)
+    right = jnp.concatenate(
+        [app_own_ref[quad], app_ref[quad], phi_own_ref[quad], phi_ref[quad]], axis=0
+    )
     grad = jnp.dot(mat_ref[...], right, preferred_element_type=F32)
-    base = place_ref[0] + start * 4 + pl.program_id(0) * 4
+    base = place_ref[0] + start * 4 + quad * 4
     for step in range(4):
         for i, seat in enumerate(seats):
-            place = base + step - seat
-            inside = (place >= 0) & (place < 128)
+            inside = ((base + step - seat) & -128) == 0
             own = i < 2 * levels
             keep = jnp.where(inside, scale, 0.0) if own else jnp.where(inside, 0.0, scale)
             keep = jnp.concatenate([keep, keep], axis=1)
             part = grad[i * held : (i + 1) * held, step * cross : (step + 1) * cross] * keep
-            outs[i // levels][i % levels, step] = part.astype(BF16)
+            outs[i // levels][i % levels, quad * 4 + step] = part.astype(BF16)
 
 
 def body(orbitals, region_start, kin_cross, potential, pattern):
     held, length, cross = orbitals.shape
     peers = lax.axis_size("orb")
     slabs = lax.axis_size("slab")
-    slab_id = lax.axis_index("slab").astype(jnp.int32)
-    orb_id = lax.axis_index("orb").astype(jnp.int32)
-    core, level = orb_id % 2, orb_id // 2
     levels = peers // 2
     count = held * peers
     narrow = length // peers
@@ -369,10 +401,6 @@
 
     def around(array, by):
         return send(array, lambda c, y: (0, 2 * ((y + by) % levels) + c))
-
-    near_id = jnp.where(core == 0, slab_id - 1, slab_id + 1) % slabs
-    position = (core * levels + level) * narrow + length // 2
-    place = jnp.stack([position, slab_id, near_id, level, core])
 
     pot_pairs = []
     for s in range(slabs):
@@ -383,21 +411,26 @@
                 pot_pairs.append((s * peers + k, ((s - 1) % slabs) * peers + 2 * k + 1))
     window_pot = lax.ppermute(potential, axes, pot_pairs)
 
-    def call(kernel, outs, ins, args, scratch=(), smems=0, **extra):
+    def call(kernel, outs, args, scratch=(), smems=0, grid=(1,), slow=()):
+        def spec(item, far):
+            return pl.BlockSpec(item.shape, lambda t: (0,) * len(item.shape)) if far else vmem()
+
+        first, arrays = args[:smems], args[smems:]
+        far = [any(item is other for other in slow) for item in arrays]
         return pl.pallas_call(
             kernel,
-            grid=(1,),
+            grid=grid,
             out_shape=outs,
-            in_specs=[smem()] * smems + ins,
-            out_specs=jax.tree.map(lambda item: fixed(*item.shape), outs),
+            in_specs=[smem()] * smems + [spec(*pair) for pair in zip(arrays, far)],
+            out_specs=[spec(item, isinstance(item, jax.ShapeDtypeStruct)) for item in outs],
             scratch_shapes=list(scratch),
             compiler_params=params(),
-            **extra,
-        )(*args)
-
-    def whole(arrays):
-        return [fixed(*item.shape) for item in arrays]
-
+        )(*first, *[item if away else near_core(item) for item, away in zip(arrays, far)])
+
+    def far_off(array):
+        return pltpu.with_memory_space_constraint(array, pltpu.HBM)
+
+    orbitals, region_start = far_off(orbitals), far_off(region_start)
     part = held // 2
     scratch = pltpu.VMEM((cross // 128, length * part, 128), F32)
     deep = [last - first + (1 if i == 0 else 0) for i, (first, last) in enumerate(spans(cuts))]
@@ -406,16 +439,12 @@
         functools.partial(spread_kernel, cuts=cuts),
         grid=(2,),
         out_shape=[shaped((2, rows, held, cross)) for rows in deep for _ in range(levels)],
-        in_specs=[smem(), smem(), by_part],
-        out_specs=[
-            pl.BlockSpec((2, rows, part, cross), lambda t: (0, 0, t, 0))
-            for rows in deep
-            for _ in range(levels)
-        ],
+        in_specs=[smem(), by_part],
+        out_specs=[vmem()] * (len(deep) * levels),
         scratch_shapes=[scratch],
         compiler_params=params(),
         name="spread",
-    )(region_start, place, orbitals)
+    )(region_start, orbitals)
     across = pltpu.VMEM((count, cross), F32)
     home_sides, near_sides = [], []
     for which in range(chunks):
@@ -427,31 +456,18 @@
         home_sides.append((same, swapped(other)))
 
     def chunk_args(sides, which):
-        arrays = list(sides[which])
-        specs = whole(arrays)
-        if which > 0:
-            for side in range(2):
-                for back_by in (2, 1):
-                    item = sides[which - 1][side]
-                    at = item.shape[1] - back_by
-                    arrays.append(item)
-                    specs.append(
-                        pl.BlockSpec(
-                            (levels, 1, held, cross), lambda t, at=at: (0, at, 0, 0)
-                        )
-                    )
-        return arrays, specs
+        return list(sides[which]) + (list(sides[which - 1]) if which > 0 else [])
 
     fields = [
         shaped((cuts[i + 1] - cuts[i], count, 4 * cross)) for i in range(chunks)
     ]
-    seat = shaped((count, 128), F32)
+    seat = jax.ShapeDtypeStruct((count, 128), jnp.int32)
     homes, nears = [], []
     home_off = near_off = pair = table = None
     for which in range(chunks):
-        arrays, specs = chunk_args(home_sides, which)
+        arrays = chunk_args(home_sides, which)
         fixed_args = [window_pot, kin_cross]
-        outs = [fields[which]] * 2 + [shaped((2 * count, count), F32)]
+        outs = [fields[which]] * 2 + [jax.ShapeDtypeStruct((2 * count, count), F32)]
         if which == 0:
             outs.append(seat)
             more = []
@@ -460,10 +476,9 @@
         result = call(
             functools.partial(own_kernel, which=which, cuts=cuts),
             outs,
-            whole(fixed_args) + specs + whole(more),
-            (place, *fixed_args, *arrays, *more),
+            [*fixed_args, *arrays, *more],
             [across],
-            1,
+            slow=[home_off, pair],
         )
         homes.append(result[:2])
         pair = result[2]
@@ -472,7 +487,7 @@
     packed = (2, 5 * 16, 2 * count)
     table_shape = (2, 2 * count + BLOCK, 2 * count)
     for which in range(chunks):
-        arrays, specs = chunk_args(near_sides, which)
+        arrays = chunk_args(near_sides, which)
         fixed_args = [window_pot, kin_cross]
         last = which == chunks - 1
         more = list(homes[which])
@@ -492,10 +507,10 @@
         result = call(
             functools.partial(near_kernel, which=which, cuts=cuts, scale=1.0 / (length * cross)),
             outs,
-            whole(fixed_args) + specs + whole(more),
-            (place, pattern, *fixed_args, *arrays, *more),
+            (pattern.T, *fixed_args, *arrays, *more),
             temp,
-            2,
+            1,
+            slow=[near_off, pair],
         )
         nears.append(result[:2])
         rest = result[2:]
@@ -511,31 +526,34 @@
         total = total + item.astype(F32)
     held_sum = total[:, :, :count] + back(total[:, :, count:].astype(PARTIAL)).astype(F32)
     done = (held_sum + swapped(held_sum)).astype(BF16)
-    dones = jnp.stack([done] + [around(done, by) for by in range(1, levels)])
-    passed = onward(dones)
+    dones = [done] + [around(done, by) for by in range(1, levels)]
+    passed = [
+        send(
+            done,
+            lambda c, y, by=by: (
+                (1, 2 * ((y + by) % levels)) if c == 0 else (-1, 2 * ((y + by) % levels) + 1)
+            ),
+        )
+        for by in range(levels)
+    ]
     mat = call(
-        unpack_kernel,
-        shaped((2 * count, 4 * count)),
-        whole([dones, passed]),
-        (place, pattern, dones, passed),
-        (),
-        2,
-    )
+        unpack_kernel, [shaped((2 * count, 4 * count))], (pattern.T, *dones, *passed), (), 1
+    )[0]
     got = []
     for which in range(chunks):
         wide = 4 * (cuts[which + 1] - cuts[which])
         more = [home_off, near_off, mat, *homes[which], *nears[which]]
-        by_quad = pl.BlockSpec((1, count, 4 * cross), lambda t: (t, 0, 0))
-        own_same, own_other, near_same, near_other = pl.pallas_call(
+        own_same, own_other, near_same, near_other = call(
             functools.partial(
                 gradient_kernel, start=cuts[which], scale=1.0 / (pattern.shape[1] * BLOCK)
             ),
-            grid=(wide // 4,),
-            out_shape=[shaped((levels, wide, held, cross))] * 4,
-            in_specs=[smem()] + whole(more[:3]) + [by_quad] * 4,
-            out_specs=[pl.BlockSpec((levels, 4, held, cross), lambda t: (0, t, 0, 0))] * 4,
-            compiler_params=params(),
-        )(place, *more)
+            [shaped((levels, wide, held, cross))] * 4,
+            [*more],
+            (),
+            0,
+            (wide // 4,),
+            [home_off, near_off],
+        )
         first, second = back(near_same), across_up(near_other)
         given = swapped(own_other)
         first = own_same + first
@@ -545,14 +563,13 @@
     return pl.pallas_call(
         functools.partial(collect_kernel, cuts=cuts),
         grid=(2,),
-        out_shape=shaped(orbitals.shape),
-        in_specs=[smem(), smem()]
-        + [pl.BlockSpec((2, item.shape[1], part, cross), lambda t: (0, 0, t, 0)) for item in got],
+        out_shape=jax.ShapeDtypeStruct(orbitals.shape, BF16),
+        in_specs=[smem()] + [vmem()] * len(got),
         out_specs=by_part,
         scratch_shapes=[scratch],
         compiler_params=params(),
         name="collect",
-    )(region_start, place, *got)
+    )(region_start, *map(near_core, got))
 
 
 def solution(mesh):

time: 191 us -> 175 us (0.916)
  Pallas kernels: 49.8 us -> 27 us
  waiting for transfers between devices: 86.1 us -> 105 us
  local copies, waits for them, and re-layouts: 6.33 us -> 0.35 us
  other arithmetic: 4.76 us -> 1.38 us
  starting transfers between devices: 43.1 us -> 40.6 us
    pallas_call x7, Pallas kernels: 40.9 us -> 19 us  [call(): pl.pallas_call(kernel, grid=grid, out_shape=outs, in_specs=[smem()] * sme...]
    ppermute x33 -> x36, waiting for transfers between devices: 86.1 us -> 105 us  [send(): return lax.ppermute(array, axes, pairs)]
    unnamed x35 -> x4, local copies, waits for them, and re-layouts: 3.42 us -> 0.01 us
    ppermute x33 -> x36, starting transfers between devices: 35.3 us -> 32.8 us  [send(): return lax.ppermute(array, axes, pairs)]
    slice x8, local copies, waits for them, and re-layouts: 2.15 us -> 0.17 us  [body(): other = jnp.stack([item[1] for item in got])]
  transfers between devices with their start and end apart: 34 -> 37, of which waited for: 20 -> 22; matrix products, arithmetic and copies ran while one was open for 4% -> 1% of each run, Pallas kernels for 15% -> 9%
where the time goes in v1:
time: 175 us
  waiting for transfers between devices  105 us (60%)
  starting transfers between devices  40.6 us (23%)
  Pallas kernels  27 us (15%)
    ppermute x36, waiting for transfers between devices, send(): return lax.ppermute(array, axes, pairs)  105 us
    ppermute x36, starting transfers between devices, send(): return lax.ppermute(array, axes, pairs)  32.8 us
    pallas_call x7, Pallas kernels, call(): pl.pallas_call(kernel, grid=grid, out_shape=outs, in_specs=[smem()] * sme...  19 us
    ppermute x1, starting transfers between devices, body(): window_pot = lax.ppermute(potential, axes, pot_pairs)  7.78 us
    pallas_call x1, Pallas kernels, body(): pl.pallas_call(functools.partial(spread_kernel, cuts=cuts), grid=(2,), ou...  4 us
    pallas_call x1, Pallas kernels, body(): pl.pallas_call(functools.partial(collect_kernel, cuts=cuts), grid=(2,), o...  3.97 us
  transfers between devices with their start and end apart: 37, of which 22 were waited for; matrix products, arithmetic and copies ran while one was open for 1% of the time, Pallas kernels for 9%

profile of v1, /device:TPU:1, one launch (start us, length us, event | category | flops | bytes accessed | tf_op | source)
XLA Modules:
  0.0 174.7 jit_solution(5148837587334998857)
XLA Ops:
  0.0 7.8 %collective-permute-start = (f32[16,256]{1,0:T(8,128)}, f32[16,256]{1,0:T(8,128)S(1)}, u32[]{:S(2)}, u32[]{:S(2)}) collective-permute-start(f32[16,256]{1,0:T(8,128)} %param.8), channel_id=1, source_target_pairs={{0,121},{1,123},{2,125},{3,127},{4,0},{5,2},{6,4},{7,6},{8,1},{9,3... | collective-permute-start | bytes 49160 | tf_op jit(solution)/shard_map/ppermute | solution.py:412
  7.8 4.0 %spread.1 = (bf16[2,11,32,256]{3,2,1,0:T(8,128)(2,1)S(1)}, bf16[2,11,32,256]{3,2,1,0:T(8,128)(2,1)S(1)}, bf16[2,11,32,256]{3,2,1,0:T(8,128)(2,1)S(1)}, bf16[2,11...) custom-call(s32[32]{0:T(128)} %start_ref.3, ...), custom_call_target="tpu_custom_call" | custom-call | tf_op jit(solution)/shard_map/spread/pallas_call | solution.py:438
  11.8 2.1 %collective-permute-start.7 = (bf16[2,8,32,256]{3,2,1,0:T(8,128)(2,1)S(1)}, bf16[2,8,32,256]{3,2,1,0:T(8,128)(2,1)S(1)}, u32[]{:S(2)}, u32[]{:S(2)}) collective-permute-start(bf16[2,8,32,256]{3,2,1,0:T(8,128)(2,1)S(1)} %get-tuple-element.47), channel_id=1, source_target_pairs={{0,2},{1,3},{2,4},{3,5},{4,6},{5,7},{6,0},{7,1},{8,10},{9,11},{10,... | collective-permute-start | bytes 786440 | tf_op jit(solution)/shard_map/ppermute | solution.py:388
  13.9 2.5 %collective-permute-start.9 = (bf16[2,8,32,256]{3,2,1,0:T(8,128)(2,1)S(1)}, bf16[2,8,32,256]{3,2,1,0:T(8,128)(2,1)S(1)}, u32[]{:S(2)}, u32[]{:S(2)}) collective-permute-start(bf16[2,8,32,256]{3,2,1,0:T(8,128)(2,1)S(1)} %get-tuple-element.49), channel_id=1, source_target_pairs={{0,6},{1,7},{2,0},{3,1},{4,2},{5,3},{6,4},{7,5},{8,14},{9,15},{10,... | collective-permute-start | bytes 786440 | tf_op jit(solution)/shard_map/ppermute | solution.py:388
  16.4 10.6 %collective-permute-done.7 = bf16[2,8,32,256]{3,2,1,0:T(8,128)(2,1)S(1)} collective-permute-done((bf16[2,8,32,256]{3,2,1,0:T(8,128)(2,1)S(1)}, bf16[2,8,32,256]{3,2,1,0:T(8,128)(2,1)S(1)}, u32[]{:S(2)}, u32[]{:S(2)}) %collective-permute-start.7) | collective-permute-done | bytes 262176 | tf_op jit(solution)/shard_map/ppermute | solution.py:388
  27.0 15.1 %collective-permute-done.1 = bf16[2,11,32,256]{3,2,1,0:T(8,128)(2,1)S(1)} collective-permute-done((bf16[2,11,32,256]{3,2,1,0:T(8,128)(2,1)S(1)}, bf16[2,11,32,256]{3,2,1,0:T(8,128)(2,1)S(1)}, u32[]{:S(2)}, u32[]{:S(2)}) %collective-permute-start.1) | collective-permute-done | bytes 360480 | tf_op jit(solution)/shard_map/ppermute | solution.py:388
  42.2 9.5 %collective-permute-done.3 = bf16[2,11,32,256]{3,2,1,0:T(8,128)(2,1)S(1)} collective-permute-done((bf16[2,11,32,256]{3,2,1,0:T(8,128)(2,1)S(1)}, bf16[2,11,32,256]{3,2,1,0:T(8,128)(2,1)S(1)}, u32[]{:S(2)}, u32[]{:S(2)}) %collective-permute-start.3) | collective-permute-done | bytes 360480 | tf_op jit(solution)/shard_map/ppermute | solution.py:388
  51.7 0.1 pad_maximum_fusion.1
  51.9 1.3 collective-permute-start.4
  53.3 0.1 collective-permute-start.6
  53.3 0.1 pad_maximum_fusion.refs_0_.refs_2_
  53.5 4.7 %collective-permute-start.5 = (bf16[4,11,32,256]{3,2,1,0:T(8,128)(2,1)S(1)}, bf16[4,11,32,256]{3,2,1,0:T(8,128)(2,1)S(1)}, u32[]{:S(2)}, u32[]{:S(2)}) collective-permute-start(bf16[4,11,32,256]{3,2,1,0:T(8,128)(2,1)S(1)} %pad_maximum_fusion.refs_0_.refs_2_), channel_id=1, source_target_pairs={{0,8},{1,121},{2,10},{3,123},{4,12},{5,125},{6,14},{7,127},{8,16},... | collective-permute-start | bytes 2162696 | tf_op jit(solution)/shard_map/ppermute | solution.py:388
  58.3 0.1 collective-permute-start.12
  58.5 0.5 collective-permute-start.10
  58.9 2.4 %shard_map.55 = (bf16[2,256,1024]{2,1,0:T(8,128)(2,1)S(1)}, bf16[2,256,1024]{2,1,0:T(8,128)(2,1)S(1)}, f32[512,256]{1,0:T(8,128)S(1)}, s32[256,128]{1,0:T(8,128)S(1)}) custom-call(f32[16,256]{1,0:T(8,128)S(1)} %collective-permute-done.pot_ref, bf16[256,256]{1,0:T(8,128)(2,1)S(1)} %copy-done, bf16[4,11,32,256]{3,2,1,0:T(8,128)(2,1)S(1)} %pad_maximum_fusion.refs_0_.refs_2_, ...), custom_call_target="tpu_custom_call" | custom-call | tf_op jit(solution)/shard_map/pallas_call | solution.py:420
  61.3 2.4 %shard_map.57 = (bf16[2,256,1024]{2,1,0:T(8,128)(2,1)S(1)}, bf16[2,256,1024]{2,1,0:T(8,128)(2,1)S(1)}, f32[512,256]{1,0:T(8,128)S(1)}) custom-call(f32[16,256]{1,0:T(8,128)S(1)} %collective-permute-done.pot_ref, bf16[256,256]{1,0:T(8,128)(2,1)S(1)} %copy-done, bf16[4,8,32,256]{3,2,1,0:T(8,128)(2,1)S(1)} %pad_maximum_fusion.2.refs_0_, ...), custom_call_target="tpu_custom_call" | custom-call | tf_op jit(solution)/shard_map/pallas_call | solution.py:420
  63.7 10.4 %collective-permute-done.5.refs_0_.refs_2_ = bf16[4,11,32,256]{3,2,1,0:T(8,128)(2,1)S(1)} collective-permute-done((bf16[4,11,32,256]{3,2,1,0:T(8,128)(2,1)S(1)}, bf16[4,11,32,256]{3,2,1,0:T(8,128)(2,1)S(1)}, u32[]{:S(2)}, u32[]{:S(2)}) %collective-permute-start.5) | collective-permute-done | bytes 720928 | tf_op jit(solution)/shard_map/ppermute | solution.py:388
  74.2 3.6 %shard_map.56 = (bf16[2,256,1024]{2,1,0:T(8,128)(2,1)S(1)}, bf16[2,256,1024]{2,1,0:T(8,128)(2,1)S(1)}, s32[256,128]{1,0:T(8,128)S(1)}, f32[2,512,512]{2,1,0:T(8,128)S(1)}) custom-call(s32[5,64]{1,0:T(8,128)S(1)} %bitcast.1, f32[16,256]{1,0:T(8,128)S(1)} %collective-permute-done.pot_ref, bf16[256,256]{1,0:T(8,128)(2,1)S(1)} %copy-done, ...), custom_call_target="tpu_custom_call" | custom-call | tf_op jit(solution)/shard_map/pallas_call | solution.py:420
  77.8 4.8 %collective-permute-done.10.refs_0_ = bf16[4,8,32,256]{3,2,1,0:T(8,128)(2,1)S(1)} collective-permute-done((bf16[4,8,32,256]{3,2,1,0:T(8,128)(2,1)S(1)}, bf16[4,8,32,256]{3,2,1,0:T(8,128)(2,1)S(1)}, u32[]{:S(2)}, u32[]{:S(2)}) %collective-permute-start.10) | collective-permute-done | bytes 524320 | tf_op jit(solution)/shard_map/ppermute | solution.py:388
  82.5 0.4 collective-permute-done.11.refs_1_
  82.9 3.9 %shard_map.58 = (bf16[2,256,1024]{2,1,0:T(8,128)(2,1)S(1)}, bf16[2,256,1024]{2,1,0:T(8,128)(2,1)S(1)}, bf16[2,80,512]{2,1,0:T(8,128)(2,1)S(1)}, bf16[2,80,512]{2...) custom-call(s32[5,64]{1,0:T(8,128)S(1)} %bitcast.2, ...), custom_call_target="tpu_custom_call" | custom-call | tf_op jit(solution)/shard_map/pallas_call | solution.py:420
  86.8 0.1 collective-permute-start.13
  86.9 2.4 %collective-permute-start.14 = (bf16[2,80,512]{2,1,0:T(8,128)(2,1)S(1)}, bf16[2,80,512]{2,1,0:T(8,128)(2,1)S(1)}, u32[]{:S(2)}, u32[]{:S(2)}) collective-permute-start(bf16[2,80,512]{2,1,0:T(8,128)(2,1)S(1)} %get-tuple-element.57), channel_id=1, source_target_pairs={{0,4},{1,5},{2,6},{3,7},{4,0},{5,1},{6,2},{7,3},{8,12},{9,13},{10,... | collective-permute-start | bytes 491528 | tf_op jit(solution)/shard_map/ppermute | solution.py:388
  89.3 0.3 collective-permute-start.15
  89.6 4.5 %collective-permute-done.13 = bf16[2,80,512]{2,1,0:T(8,128)(2,1)S(1)} collective-permute-done((bf16[2,80,512]{2,1,0:T(8,128)(2,1)S(1)}, bf16[2,80,512]{2,1,0:T(8,128)(2,1)S(1)}, u32[]{:S(2)}, u32[]{:S(2)}) %collective-permute-start.13) | collective-permute-done | bytes 163872 | tf_op jit(solution)/shard_map/ppermute | solution.py:388
  94.1 0.9 collective-permute-done.15
  95.0 0.1 convert_add_fusion
  95.1 0.6 collective-permute-start.16
  95.6 7.5 %collective-permute-done.16 = bf16[2,80,256]{2,1,0:T(8,128)(2,1)S(1)} collective-permute-done((bf16[2,80,256]{2,1,0:T(8,128)(2,1)S(1)}, bf16[2,80,256]{2,1,0:T(8,128)(2,1)S(1)}, u32[]{:S(2)}, u32[]{:S(2)}) %collective-permute-start.16) | collective-permute-done | bytes 81952 | tf_op jit(solution)/shard_map/ppermute | solution.py:388
  103.2 1.6 collective-permute-start.17
  104.8 1.0 collective-permute-done.17
  105.8 7.3 %collective-permute-start.24 = (bf16[2,80,256]{2,1,0:T(8,128)(2,1)S(1)}, bf16[2,80,256]{2,1,0:T(8,128)(2,1)S(1)}, u32[]{:S(2)}, u32[]{:S(2)}) collective-permute-start(bf16[2,80,256]{2,1,0:T(8,128)(2,1)S(1)} %add_convert_fusion.rest_0_), channel_id=1, source_target_pairs={{0,14},{1,127},{2,8},{3,121},{4,10},{5,123},{6,12},{7,125},{8,22},... | collective-permute-start | bytes 245768 | tf_op jit(solution)/shard_map/ppermute | solution.py:388
  113.1 0.8 collective-permute-start.20
  113.9 0.7 collective-permute-done.24.rest_7_
  114.6 1.0 collective-permute-start.19
  115.5 3.9 %collective-permute-done.23.rest_6_ = bf16[2,80,256]{2,1,0:T(8,128)(2,1)S(1)} collective-permute-done((bf16[2,80,256]{2,1,0:T(8,128)(2,1)S(1)}, bf16[2,80,256]{2,1,0:T(8,128)(2,1)S(1)}, u32[]{:S(2)}, u32[]{:S(2)}) %collective-permute-start.23) | collective-permute-done | bytes 81952 | tf_op jit(solution)/shard_map/ppermute | solution.py:388
  119.4 2.2 %collective-permute-done.19.rest_2_ = bf16[2,80,256]{2,1,0:T(8,128)(2,1)S(1)} collective-permute-done((bf16[2,80,256]{2,1,0:T(8,128)(2,1)S(1)}, bf16[2,80,256]{2,1,0:T(8,128)(2,1)S(1)}, u32[]{:S(2)}, u32[]{:S(2)}) %collective-permute-start.19) | collective-permute-done | bytes 81952 | tf_op jit(solution)/shard_map/ppermute | solution.py:388
  121.6 2.3 %collective-permute-done.18.rest_1_ = bf16[2,80,256]{2,1,0:T(8,128)(2,1)S(1)} collective-permute-done((bf16[2,80,256]{2,1,0:T(8,128)(2,1)S(1)}, bf16[2,80,256]{2,1,0:T(8,128)(2,1)S(1)}, u32[]{:S(2)}, u32[]{:S(2)}) %collective-permute-start.18) | collective-permute-done | bytes 81952 | tf_op jit(solution)/shard_map/ppermute | solution.py:388
  123.9 1.6 shard_map.59.mat_ref
  125.5 2.6 %shard_map.61 = (bf16[4,8,32,256]{3,2,1,0:T(8,128)(2,1)S(1)}, bf16[4,8,32,256]{3,2,1,0:T(8,128)(2,1)S(1)}, bf16[4,8,32,256]{3,2,1,0:T(8,128)(2,1)S(1)}, bf16[4,8,32,256]{3,2,1,0:T(8,128)(2,1)S(1)}) custom-call(s32[256,128]{1,0:T(8,128)S(1)} %get-tuple-element.42.refs_4_.off_own_ref, s32[256,128]{1,0:T(8,128)S(1)} %get-tuple-element.45.refs_7_.off_near_ref, ...), custom_call_target="tpu_custom_call" | custom-call | tf_op jit(solution)/shard_map/pallas_call | solution.py:420
  128.1 0.1 collective-permute-start.31
  128.2 2.9 %collective-permute-start.32 = (bf16[4,8,32,256]{3,2,1,0:T(8,128)(2,1)S(1)}, bf16[4,8,32,256]{3,2,1,0:T(8,128)(2,1)S(1)}, u32[]{:S(2)}, u32[]{:S(2)}) collective-permute-start(bf16[4,8,32,256]{3,2,1,0:T(8,128)(2,1)S(1)} %get-tuple-element.69), channel_id=1, source_target_pairs={{0,1},{1,0},{2,3},{3,2},{4,5},{5,4},{6,7},{7,6},{8,9},{9,8},{10,11... | collective-permute-start | bytes 1572872 | tf_op jit(solution)/shard_map/ppermute | solution.py:388
  131.1 0.5 collective-permute-start.33
  131.6 2.6 %shard_map.60 = (bf16[4,8,32,256]{3,2,1,0:T(8,128)(2,1)S(1)}, bf16[4,8,32,256]{3,2,1,0:T(8,128)(2,1)S(1)}, bf16[4,8,32,256]{3,2,1,0:T(8,128)(2,1)S(1)}, bf16[4,8,32,256]{3,2,1,0:T(8,128)(2,1)S(1)}) custom-call(s32[256,128]{1,0:T(8,128)S(1)} %get-tuple-element.42.refs_4_.off_own_ref, s32[256,128]{1,0:T(8,128)S(1)} %get-tuple-element.45.refs_7_.off_near_ref, ...), custom_call_target="tpu_custom_call" | custom-call | tf_op jit(solution)/shard_map/pallas_call | solution.py:420
  134.2 0.2 collective-permute-start.25
  134.4 2.0 %collective-permute-start.26 = (bf16[4,8,32,256]{3,2,1,0:T(8,128)(2,1)S(1)}, bf16[4,8,32,256]{3,2,1,0:T(8,128)(2,1)S(1)}, u32[]{:S(2)}, u32[]{:S(2)}) collective-permute-start(bf16[4,8,32,256]{3,2,1,0:T(8,128)(2,1)S(1)} %get-tuple-element.63), channel_id=1, source_target_pairs={{0,1},{1,0},{2,3},{3,2},{4,5},{5,4},{6,7},{7,6},{8,9},{9,8},{10,11... | collective-permute-start | bytes 1572872 | tf_op jit(solution)/shard_map/ppermute | solution.py:388
  136.4 3.1 %collective-permute-done.31 = bf16[4,8,32,256]{3,2,1,0:T(8,128)(2,1)S(1)} collective-permute-done((bf16[4,8,32,256]{3,2,1,0:T(8,128)(2,1)S(1)}, bf16[4,8,32,256]{3,2,1,0:T(8,128)(2,1)S(1)}, u32[]{:S(2)}, u32[]{:S(2)}) %collective-permute-start.31) | collective-permute-done | bytes 524320 | tf_op jit(solution)/shard_map/ppermute | solution.py:388
  139.5 0.2 add.34
  139.8 4.6 %collective-permute-done.33 = bf16[4,8,32,256]{3,2,1,0:T(8,128)(2,1)S(1)} collective-permute-done((bf16[4,8,32,256]{3,2,1,0:T(8,128)(2,1)S(1)}, bf16[4,8,32,256]{3,2,1,0:T(8,128)(2,1)S(1)}, u32[]{:S(2)}, u32[]{:S(2)}) %collective-permute-start.33) | collective-permute-done | bytes 524320 | tf_op jit(solution)/shard_map/ppermute | solution.py:388
  144.4 0.2 add.35
  144.7 0.1 collective-permute-start.34
  144.8 0.6 collective-permute-start.35
  145.4 5.3 %collective-permute-done.25 = bf16[4,8,32,256]{3,2,1,0:T(8,128)(2,1)S(1)} collective-permute-done((bf16[4,8,32,256]{3,2,1,0:T(8,128)(2,1)S(1)}, bf16[4,8,32,256]{3,2,1,0:T(8,128)(2,1)S(1)}, u32[]{:S(2)}, u32[]{:S(2)}) %collective-permute-start.25) | collective-permute-done | bytes 524320 | tf_op jit(solution)/shard_map/ppermute | solution.py:388
  150.8 0.2 add.32
  151.0 4.6 %collective-permute-done.27 = bf16[4,8,32,256]{3,2,1,0:T(8,128)(2,1)S(1)} collective-permute-done((bf16[4,8,32,256]{3,2,1,0:T(8,128)(2,1)S(1)}, bf16[4,8,32,256]{3,2,1,0:T(8,128)(2,1)S(1)}, u32[]{:S(2)}, u32[]{:S(2)}) %collective-permute-start.27) | collective-permute-done | bytes 524320 | tf_op jit(solution)/shard_map/ppermute | solution.py:388
  155.6 0.2 add.33
  155.9 0.1 collective-permute-start.28
  156.0 0.6 collective-permute-start.29
  156.6 1.8 %collective-permute-done.34.rest_5_ = bf16[2,8,32,256]{3,2,1,0:T(8,128)(2,1)S(1)} collective-permute-done((bf16[2,8,32,256]{3,2,1,0:T(8,128)(2,1)S(1)}, bf16[2,8,32,256]{3,2,1,0:T(8,128)(2,1)S(1)}, u32[]{:S(2)}, u32[]{:S(2)}) %collective-permute-start.34) | collective-permute-done | bytes 262176 | tf_op jit(solution)/shard_map/ppermute | solution.py:388
  158.4 0.5 collective-permute-start.30
  158.9 0.6 collective-permute-done.36.rest_7_
  159.6 10.0 %collective-permute-done.28.rest_1_ = bf16[2,8,32,256]{3,2,1,0:T(8,128)(2,1)S(1)} collective-permute-done((bf16[2,8,32,256]{3,2,1,0:T(8,128)(2,1)S(1)}, bf16[2,8,32,256]{3,2,1,0:T(8,128)(2,1)S(1)}, u32[]{:S(2)}, u32[]{:S(2)}) %collective-permute-start.28) | collective-permute-done | bytes 262176 | tf_op jit(solution)/shard_map/ppermute | solution.py:388
  169.6 1.1 collective-permute-done.30.rest_3_
  170.7 4.0 %collect.1 = bf16[32,128,256]{2,1,0:T(8,128)(2,1)} custom-call(s32[32]{0:T(128)} %start_ref.3, bf16[2,8,32,256]{3,2,1,0:T(8,128)(2,1)S(1)} %get-tuple-element.103.rest_0_, bf16[2,8,32,256]{3,2,1,0:T(8,128)(2,1)S(1)} %collective-permute-done.28.rest_1_, bf16[2,8,32,256]{3,2,1,0:T(8,128)(2,1)S(1)} %collective-permute-done.29.rest_2_, ...), custom_call_target="tpu_custom_call" | custom-call | tf_op jit(solution)/shard_map/collect/pallas_call | solution.py:563
  (54 shorter events, 0.8 us)
Async XLA Ops:
  0.0 58.5 %collective-permute-start = (f32[16,256]{1,0:T(8,128)}, f32[16,256]{1,0:T(8,128)S(1)}, u32[]{:S(2)}, u32[]{:S(2)}) collective-permute-start(f32[16,256]{1,0:T(8,128)} %param.8), channel_id=1, source_target_pairs={{0,121},{1,123},{2,125},{3,127},{4,0},{5,2},{6,4},{7,6},{8,1},{9,3... | collective-permute-start | bytes 49160 | tf_op jit(solution)/shard_map/ppermute | solution.py:412
  11.8 15.2 %collective-permute-start.7 = (bf16[2,8,32,256]{3,2,1,0:T(8,128)(2,1)S(1)}, bf16[2,8,32,256]{3,2,1,0:T(8,128)(2,1)S(1)}, u32[]{:S(2)}, u32[]{:S(2)}) collective-permute-start(bf16[2,8,32,256]{3,2,1,0:T(8,128)(2,1)S(1)} %get-tuple-element.47), channel_id=1, source_target_pairs={{0,2},{1,3},{2,4},{3,5},{4,6},{5,7},{6,0},{7,1},{8,10},{9,11},{10,... | collective-permute-start | bytes 786440 | tf_op jit(solution)/shard_map/ppermute | solution.py:388
  13.9 39.3 %collective-permute-start.8 = (bf16[2,8,32,256]{3,2,1,0:T(8,128)(2,1)S(1)}, bf16[2,8,32,256]{3,2,1,0:T(8,128)(2,1)S(1)}, u32[]{:S(2)}, u32[]{:S(2)}) collective-permute-start(bf16[2,8,32,256]{3,2,1,0:T(8,128)(2,1)S(1)} %get-tuple-element.48), channel_id=1, source_target_pairs={{0,4},{1,5},{2,6},{3,7},{4,0},{5,1},{6,2},{7,3},{8,12},{9,13},{10,... | collective-permute-start | bytes 786440 | tf_op jit(solution)/shard_map/ppermute | solution.py:388
  13.9 39.3 %collective-permute-start.9 = (bf16[2,8,32,256]{3,2,1,0:T(8,128)(2,1)S(1)}, bf16[2,8,32,256]{3,2,1,0:T(8,128)(2,1)S(1)}, u32[]{:S(2)}, u32[]{:S(2)}) collective-permute-start(bf16[2,8,32,256]{3,2,1,0:T(8,128)(2,1)S(1)} %get-tuple-element.49), channel_id=1, source_target_pairs={{0,6},{1,7},{2,0},{3,1},{4,2},{5,3},{6,4},{7,5},{8,14},{9,15},{10,... | collective-permute-start | bytes 786440 | tf_op jit(solution)/shard_map/ppermute | solution.py:388
  16.4 25.8 %collective-permute-start.1 = (bf16[2,11,32,256]{3,2,1,0:T(8,128)(2,1)S(1)}, bf16[2,11,32,256]{3,2,1,0:T(8,128)(2,1)S(1)}, u32[]{:S(2)}, u32[]{:S(2)}) collective-permute-start(bf16[2,11,32,256]{3,2,1,0:T(8,128)(2,1)S(1)} %get-tuple-element.39), channel_id=1, source_target_pairs={{0,2},{1,3},{2,4},{3,5},{4,6},{5,7},{6,0},{7,1},{8,10},{9,11},{10,... | collective-permute-start | bytes 1081352 | tf_op jit(solution)/shard_map/ppermute | solution.py:388
  27.0 15.2 %collective-permute-start.2 = (bf16[2,11,32,256]{3,2,1,0:T(8,128)(2,1)S(1)}, bf16[2,11,32,256]{3,2,1,0:T(8,128)(2,1)S(1)}, u32[]{:S(2)}, u32[]{:S(2)}) collective-permute-start(bf16[2,11,32,256]{3,2,1,0:T(8,128)(2,1)S(1)} %get-tuple-element.40), channel_id=1, source_target_pairs={{0,4},{1,5},{2,6},{3,7},{4,0},{5,1},{6,2},{7,3},{8,12},{9,13},{10,... | collective-permute-start | bytes 1081352 | tf_op jit(solution)/shard_map/ppermute | solution.py:388
  42.1 9.6 %collective-permute-start.3 = (bf16[2,11,32,256]{3,2,1,0:T(8,128)(2,1)S(1)}, bf16[2,11,32,256]{3,2,1,0:T(8,128)(2,1)S(1)}, u32[]{:S(2)}, u32[]{:S(2)}) collective-permute-start(bf16[2,11,32,256]{3,2,1,0:T(8,128)(2,1)S(1)} %get-tuple-element.41), channel_id=1, source_target_pairs={{0,6},{1,7},{2,0},{3,1},{4,2},{5,3},{6,4},{7,5},{8,14},{9,15},{10,... | collective-permute-start | bytes 1081352 | tf_op jit(solution)/shard_map/ppermute | solution.py:388
  51.9 7.1 %collective-permute-start.4 = (bf16[4,11,32,256]{3,2,1,0:T(8,128)(2,1)S(1)}, bf16[4,11,32,256]{3,2,1,0:T(8,128)(2,1)S(1)}, u32[]{:S(2)}, u32[]{:S(2)}) collective-permute-start(bf16[4,11,32,256]{3,2,1,0:T(8,128)(2,1)S(1)} %pad_maximum_fusion.1), channel_id=1, source_target_pairs={{0,1},{1,0},{2,3},{3,2},{4,5},{5,4},{6,7},{7,6},{8,9},{9,8},{10,11... | collective-permute-start | bytes 2162696 | tf_op jit(solution)/shard_map/ppermute | solution.py:388
  53.2 5.7 %copy-start = (bf16[256,256]{1,0:T(8,128)(2,1)S(1)}, bf16[256,256]{1,0:T(8,128)(2,1)}, u32[]{:S(2)}) copy-start(bf16[256,256]{1,0:T(8,128)(2,1)} %kin_ref.7) | copy-start | bytes 393220
  53.3 20.9 %collective-permute-start.6 = (bf16[4,11,32,256]{3,2,1,0:T(8,128)(2,1)S(1)}, bf16[4,11,32,256]{3,2,1,0:T(8,128)(2,1)S(1)}, u32[]{:S(2)}, u32[]{:S(2)}) collective-permute-start(bf16[4,11,32,256]{3,2,1,0:T(8,128)(2,1)S(1)} %pad_maximum_fusion.1), channel_id=1, source_target_pairs={{0,121},{1,8},{2,123},{3,10},{4,125},{5,12},{6,127},{7,14},{8,1},{... | collective-permute-start | bytes 2162696 | tf_op jit(solution)/shard_map/ppermute | solution.py:388
  53.5 20.7 %collective-permute-start.5 = (bf16[4,11,32,256]{3,2,1,0:T(8,128)(2,1)S(1)}, bf16[4,11,32,256]{3,2,1,0:T(8,128)(2,1)S(1)}, u32[]{:S(2)}, u32[]{:S(2)}) collective-permute-start(bf16[4,11,32,256]{3,2,1,0:T(8,128)(2,1)S(1)} %pad_maximum_fusion.refs_0_.refs_2_), channel_id=1, source_target_pairs={{0,8},{1,121},{2,10},{3,123},{4,12},{5,125},{6,14},{7,127},{8,16},... | collective-permute-start | bytes 2162696 | tf_op jit(solution)/shard_map/ppermute | solution.py:388
  58.3 3.0 %collective-permute-start.12 = (bf16[4,8,32,256]{3,2,1,0:T(8,128)(2,1)S(1)}, bf16[4,8,32,256]{3,2,1,0:T(8,128)(2,1)S(1)}, u32[]{:S(2)}, u32[]{:S(2)}) collective-permute-start(bf16[4,8,32,256]{3,2,1,0:T(8,128)(2,1)S(1)} %pad_maximum_fusion.3), channel_id=1, source_target_pairs={{0,1},{1,0},{2,3},{3,2},{4,5},{5,4},{6,7},{7,6},{8,9},{9,8},{10,11... | collective-permute-start | bytes 1572872 | tf_op jit(solution)/shard_map/ppermute | solution.py:388
  58.4 15.7 %copy-start.1 = (s32[64,5]{0,1:T(8,128)S(1)}, s32[64,5]{0,1:T(8,128)}, u32[]{:S(2)}) copy-start(s32[64,5]{0,1:T(8,128)} %param.9) | copy-start | bytes 3844
  58.5 24.1 %collective-permute-start.10 = (bf16[4,8,32,256]{3,2,1,0:T(8,128)(2,1)S(1)}, bf16[4,8,32,256]{3,2,1,0:T(8,128)(2,1)S(1)}, u32[]{:S(2)}, u32[]{:S(2)}) collective-permute-start(bf16[4,8,32,256]{3,2,1,0:T(8,128)(2,1)S(1)} %pad_maximum_fusion.2.refs_0_), channel_id=1, source_target_pairs={{0,8},{1,121},{2,10},{3,123},{4,12},{5,125},{6,14},{7,127},{8,16},... | collective-permute-start | bytes 1572872 | tf_op jit(solution)/shard_map/ppermute | solution.py:388
  58.9 24.0 %collective-permute-start.11 = (bf16[4,8,32,256]{3,2,1,0:T(8,128)(2,1)S(1)}, bf16[4,8,32,256]{3,2,1,0:T(8,128)(2,1)S(1)}, u32[]{:S(2)}, u32[]{:S(2)}) collective-permute-start(bf16[4,8,32,256]{3,2,1,0:T(8,128)(2,1)S(1)} %pad_maximum_fusion.3), channel_id=1, source_target_pairs={{0,121},{1,8},{2,123},{3,10},{4,125},{5,12},{6,127},{7,14},{8,1},{... | collective-permute-start | bytes 1572872 | tf_op jit(solution)/shard_map/ppermute | solution.py:388
  86.8 7.2 %collective-permute-start.13 = (bf16[2,80,512]{2,1,0:T(8,128)(2,1)S(1)}, bf16[2,80,512]{2,1,0:T(8,128)(2,1)S(1)}, u32[]{:S(2)}, u32[]{:S(2)}) collective-permute-start(bf16[2,80,512]{2,1,0:T(8,128)(2,1)S(1)} %get-tuple-element.56), channel_id=1, source_target_pairs={{0,2},{1,3},{2,4},{3,5},{4,6},{5,7},{6,0},{7,1},{8,10},{9,11},{10,... | collective-permute-start | bytes 491528 | tf_op jit(solution)/shard_map/ppermute | solution.py:388
  86.9 7.1 %collective-permute-start.14 = (bf16[2,80,512]{2,1,0:T(8,128)(2,1)S(1)}, bf16[2,80,512]{2,1,0:T(8,128)(2,1)S(1)}, u32[]{:S(2)}, u32[]{:S(2)}) collective-permute-start(bf16[2,80,512]{2,1,0:T(8,128)(2,1)S(1)} %get-tuple-element.57), channel_id=1, source_target_pairs={{0,4},{1,5},{2,6},{3,7},{4,0},{5,1},{6,2},{7,3},{8,12},{9,13},{10,... | collective-permute-start | bytes 491528 | tf_op jit(solution)/shard_map/ppermute | solution.py:388
  89.3 5.6 %collective-permute-start.15 = (bf16[2,80,512]{2,1,0:T(8,128)(2,1)S(1)}, bf16[2,80,512]{2,1,0:T(8,128)(2,1)S(1)}, u32[]{:S(2)}, u32[]{:S(2)}) collective-permute-start(bf16[2,80,512]{2,1,0:T(8,128)(2,1)S(1)} %get-tuple-element.58), channel_id=1, source_target_pairs={{0,6},{1,7},{2,0},{3,1},{4,2},{5,3},{6,4},{7,5},{8,14},{9,15},{10,... | collective-permute-start | bytes 491528 | tf_op jit(solution)/shard_map/ppermute | solution.py:388
  95.1 8.1 %collective-permute-start.16 = (bf16[2,80,256]{2,1,0:T(8,128)(2,1)S(1)}, bf16[2,80,256]{2,1,0:T(8,128)(2,1)S(1)}, u32[]{:S(2)}, u32[]{:S(2)}) collective-permute-start(bf16[2,80,256]{2,1,0:T(8,128)(2,1)S(1)} %slice.169), channel_id=1, source_target_pairs={{0,120},{1,9},{2,122},{3,11},{4,124},{5,13},{6,126},{7,15},{8,0},{... | collective-permute-start | bytes 245768 | tf_op jit(solution)/shard_map/ppermute | solution.py:388
  103.2 2.6 %collective-permute-start.17 = (f32[2,80,256]{2,1,0:T(8,128)S(1)}, f32[2,80,256]{2,1,0:T(8,128)S(1)}, u32[]{:S(2)}, u32[]{:S(2)}) collective-permute-start(f32[2,80,256]{2,1,0:T(8,128)S(1)} %slice_add_fusion), channel_id=1, source_target_pairs={{0,1},{1,0},{2,3},{3,2},{4,5},{5,4},{6,7},{7,6},{8,9},{9,8},{10,11... | collective-permute-start | bytes 491528 | tf_op jit(solution)/shard_map/ppermute | solution.py:388
  105.8 8.8 %collective-permute-start.24 = (bf16[2,80,256]{2,1,0:T(8,128)(2,1)S(1)}, bf16[2,80,256]{2,1,0:T(8,128)(2,1)S(1)}, u32[]{:S(2)}, u32[]{:S(2)}) collective-permute-start(bf16[2,80,256]{2,1,0:T(8,128)(2,1)S(1)} %add_convert_fusion.rest_0_), channel_id=1, source_target_pairs={{0,14},{1,127},{2,8},{3,121},{4,10},{5,123},{6,12},{7,125},{8,22},... | collective-permute-start | bytes 245768 | tf_op jit(solution)/shard_map/ppermute | solution.py:388
  113.1 6.3 %collective-permute-start.23 = (bf16[2,80,256]{2,1,0:T(8,128)(2,1)S(1)}, bf16[2,80,256]{2,1,0:T(8,128)(2,1)S(1)}, u32[]{:S(2)}, u32[]{:S(2)}) collective-permute-start(bf16[2,80,256]{2,1,0:T(8,128)(2,1)S(1)} %add_convert_fusion.rest_0_), channel_id=1, source_target_pairs={{0,12},{1,125},{2,14},{3,127},{4,8},{5,121},{6,10},{7,123},{8,20},... | collective-permute-start | bytes 245768 | tf_op jit(solution)/shard_map/ppermute | solution.py:388
  113.1 6.3 %collective-permute-start.22 = (bf16[2,80,256]{2,1,0:T(8,128)(2,1)S(1)}, bf16[2,80,256]{2,1,0:T(8,128)(2,1)S(1)}, u32[]{:S(2)}, u32[]{:S(2)}) collective-permute-start(bf16[2,80,256]{2,1,0:T(8,128)(2,1)S(1)} %add_convert_fusion.rest_0_), channel_id=1, source_target_pairs={{0,10},{1,123},{2,12},{3,125},{4,14},{5,127},{6,8},{7,121},{8,18},... | collective-permute-start | bytes 245768 | tf_op jit(solution)/shard_map/ppermute | solution.py:388
  113.1 6.3 %collective-permute-start.21 = (bf16[2,80,256]{2,1,0:T(8,128)(2,1)S(1)}, bf16[2,80,256]{2,1,0:T(8,128)(2,1)S(1)}, u32[]{:S(2)}, u32[]{:S(2)}) collective-permute-start(bf16[2,80,256]{2,1,0:T(8,128)(2,1)S(1)} %add_convert_fusion.rest_0_), channel_id=1, source_target_pairs={{0,8},{1,121},{2,10},{3,123},{4,12},{5,125},{6,14},{7,127},{8,16},... | collective-permute-start | bytes 245768 | tf_op jit(solution)/shard_map/ppermute | solution.py:388
  113.1 6.3 %collective-permute-start.20 = (bf16[2,80,256]{2,1,0:T(8,128)(2,1)S(1)}, bf16[2,80,256]{2,1,0:T(8,128)(2,1)S(1)}, u32[]{:S(2)}, u32[]{:S(2)}) collective-permute-start(bf16[2,80,256]{2,1,0:T(8,128)(2,1)S(1)} %add_convert_fusion.rest_0_), channel_id=1, source_target_pairs={{0,6},{1,7},{2,0},{3,1},{4,2},{5,3},{6,4},{7,5},{8,14},{9,15},{10,... | collective-permute-start | bytes 245768 | tf_op jit(solution)/shard_map/ppermute | solution.py:388
  114.6 7.0 %collective-permute-start.19 = (bf16[2,80,256]{2,1,0:T(8,128)(2,1)S(1)}, bf16[2,80,256]{2,1,0:T(8,128)(2,1)S(1)}, u32[]{:S(2)}, u32[]{:S(2)}) collective-permute-start(bf16[2,80,256]{2,1,0:T(8,128)(2,1)S(1)} %add_convert_fusion.rest_0_), channel_id=1, source_target_pairs={{0,4},{1,5},{2,6},{3,7},{4,0},{5,1},{6,2},{7,3},{8,12},{9,13},{10,... | collective-permute-start | bytes 245768 | tf_op jit(solution)/shard_map/ppermute | solution.py:388
  119.4 4.5 %collective-permute-start.18 = (bf16[2,80,256]{2,1,0:T(8,128)(2,1)S(1)}, bf16[2,80,256]{2,1,0:T(8,128)(2,1)S(1)}, u32[]{:S(2)}, u32[]{:S(2)}) collective-permute-start(bf16[2,80,256]{2,1,0:T(8,128)(2,1)S(1)} %add_convert_fusion.rest_0_), channel_id=1, source_target_pairs={{0,2},{1,3},{2,4},{3,5},{4,6},{5,7},{6,0},{7,1},{8,10},{9,11},{10,... | collective-permute-start | bytes 245768 | tf_op jit(solution)/shard_map/ppermute | solution.py:388
  128.1 11.4 %collective-permute-start.31 = (bf16[4,8,32,256]{3,2,1,0:T(8,128)(2,1)S(1)}, bf16[4,8,32,256]{3,2,1,0:T(8,128)(2,1)S(1)}, u32[]{:S(2)}, u32[]{:S(2)}) collective-permute-start(bf16[4,8,32,256]{3,2,1,0:T(8,128)(2,1)S(1)} %get-tuple-element.68), channel_id=1, source_target_pairs={{0,120},{1,9},{2,122},{3,11},{4,124},{5,13},{6,126},{7,15},{8,0},{... | collective-permute-start | bytes 1572872 | tf_op jit(solution)/shard_map/ppermute | solution.py:388
  128.2 11.6 %collective-permute-start.32 = (bf16[4,8,32,256]{3,2,1,0:T(8,128)(2,1)S(1)}, bf16[4,8,32,256]{3,2,1,0:T(8,128)(2,1)S(1)}, u32[]{:S(2)}, u32[]{:S(2)}) collective-permute-start(bf16[4,8,32,256]{3,2,1,0:T(8,128)(2,1)S(1)} %get-tuple-element.69), channel_id=1, source_target_pairs={{0,1},{1,0},{2,3},{3,2},{4,5},{5,4},{6,7},{7,6},{8,9},{9,8},{10,11... | collective-permute-start | bytes 1572872 | tf_op jit(solution)/shard_map/ppermute | solution.py:388
  131.1 13.3 %collective-permute-start.33 = (bf16[4,8,32,256]{3,2,1,0:T(8,128)(2,1)S(1)}, bf16[4,8,32,256]{3,2,1,0:T(8,128)(2,1)S(1)}, u32[]{:S(2)}, u32[]{:S(2)}) collective-permute-start(bf16[4,8,32,256]{3,2,1,0:T(8,128)(2,1)S(1)} %get-tuple-element.70), channel_id=1, source_target_pairs={{0,121},{1,8},{2,123},{3,10},{4,125},{5,12},{6,127},{7,14},{8,1},{... | collective-permute-start | bytes 1572872 | tf_op jit(solution)/shard_map/ppermute | solution.py:388
  134.2 16.6 %collective-permute-start.25 = (bf16[4,8,32,256]{3,2,1,0:T(8,128)(2,1)S(1)}, bf16[4,8,32,256]{3,2,1,0:T(8,128)(2,1)S(1)}, u32[]{:S(2)}, u32[]{:S(2)}) collective-permute-start(bf16[4,8,32,256]{3,2,1,0:T(8,128)(2,1)S(1)} %get-tuple-element.62), channel_id=1, source_target_pairs={{0,120},{1,9},{2,122},{3,11},{4,124},{5,13},{6,126},{7,15},{8,0},{... | collective-permute-start | bytes 1572872 | tf_op jit(solution)/shard_map/ppermute | solution.py:388
  134.4 16.6 %collective-permute-start.26 = (bf16[4,8,32,256]{3,2,1,0:T(8,128)(2,1)S(1)}, bf16[4,8,32,256]{3,2,1,0:T(8,128)(2,1)S(1)}, u32[]{:S(2)}, u32[]{:S(2)}) collective-permute-start(bf16[4,8,32,256]{3,2,1,0:T(8,128)(2,1)S(1)} %get-tuple-element.63), channel_id=1, source_target_pairs={{0,1},{1,0},{2,3},{3,2},{4,5},{5,4},{6,7},{7,6},{8,9},{9,8},{10,11... | collective-permute-start | bytes 1572872 | tf_op jit(solution)/shard_map/ppermute | solution.py:388
  139.5 16.1 %collective-permute-start.27 = (bf16[4,8,32,256]{3,2,1,0:T(8,128)(2,1)S(1)}, bf16[4,8,32,256]{3,2,1,0:T(8,128)(2,1)S(1)}, u32[]{:S(2)}, u32[]{:S(2)}) collective-permute-start(bf16[4,8,32,256]{3,2,1,0:T(8,128)(2,1)S(1)} %get-tuple-element.64), channel_id=1, source_target_pairs={{0,121},{1,8},{2,123},{3,10},{4,125},{5,12},{6,127},{7,14},{8,1},{... | collective-permute-start | bytes 1572872 | tf_op jit(solution)/shard_map/ppermute | solution.py:388
  144.7 13.7 %collective-permute-start.34 = (bf16[2,8,32,256]{3,2,1,0:T(8,128)(2,1)S(1)}, bf16[2,8,32,256]{3,2,1,0:T(8,128)(2,1)S(1)}, u32[]{:S(2)}, u32[]{:S(2)}) collective-permute-start(bf16[2,8,32,256]{3,2,1,0:T(8,128)(2,1)S(1)} %pad_maximum_fusion.9), channel_id=1, source_target_pairs={{0,2},{1,3},{2,4},{3,5},{4,6},{5,7},{6,0},{7,1},{8,10},{9,11},{10,... | collective-permute-start | bytes 786440 | tf_op jit(solution)/shard_map/ppermute | solution.py:388
  144.8 14.2 %collective-permute-start.35 = (bf16[2,8,32,256]{3,2,1,0:T(8,128)(2,1)S(1)}, bf16[2,8,32,256]{3,2,1,0:T(8,128)(2,1)S(1)}, u32[]{:S(2)}, u32[]{:S(2)}) collective-permute-start(bf16[2,8,32,256]{3,2,1,0:T(8,128)(2,1)S(1)} %pad_maximum_fusion.10), channel_id=1, source_target_pairs={{0,4},{1,5},{2,6},{3,7},{4,0},{5,1},{6,2},{7,3},{8,12},{9,13},{10,... | collective-permute-start | bytes 786440 | tf_op jit(solution)/shard_map/ppermute | solution.py:388
  150.8 8.8 %collective-permute-start.36 = (bf16[2,8,32,256]{3,2,1,0:T(8,128)(2,1)S(1)}, bf16[2,8,32,256]{3,2,1,0:T(8,128)(2,1)S(1)}, u32[]{:S(2)}, u32[]{:S(2)}) collective-permute-start(bf16[2,8,32,256]{3,2,1,0:T(8,128)(2,1)S(1)} %pad_maximum_fusion.11), channel_id=1, source_target_pairs={{0,6},{1,7},{2,0},{3,1},{4,2},{5,3},{6,4},{7,5},{8,14},{9,15},{10,... | collective-permute-start | bytes 786440 | tf_op jit(solution)/shard_map/ppermute | solution.py:388
  155.9 13.7 %collective-permute-start.28 = (bf16[2,8,32,256]{3,2,1,0:T(8,128)(2,1)S(1)}, bf16[2,8,32,256]{3,2,1,0:T(8,128)(2,1)S(1)}, u32[]{:S(2)}, u32[]{:S(2)}) collective-permute-start(bf16[2,8,32,256]{3,2,1,0:T(8,128)(2,1)S(1)} %pad_maximum_fusion.5), channel_id=1, source_target_pairs={{0,2},{1,3},{2,4},{3,5},{4,6},{5,7},{6,0},{7,1},{8,10},{9,11},{10,... | collective-permute-start | bytes 786440 | tf_op jit(solution)/shard_map/ppermute | solution.py:388
  156.0 13.6 %collective-permute-start.29 = (bf16[2,8,32,256]{3,2,1,0:T(8,128)(2,1)S(1)}, bf16[2,8,32,256]{3,2,1,0:T(8,128)(2,1)S(1)}, u32[]{:S(2)}, u32[]{:S(2)}) collective-permute-start(bf16[2,8,32,256]{3,2,1,0:T(8,128)(2,1)S(1)} %pad_maximum_fusion.6), channel_id=1, source_target_pairs={{0,4},{1,5},{2,6},{3,7},{4,0},{5,1},{6,2},{7,3},{8,12},{9,13},{10,... | collective-permute-start | bytes 786440 | tf_op jit(solution)/shard_map/ppermute | solution.py:388
  158.4 12.3 %collective-permute-start.30 = (bf16[2,8,32,256]{3,2,1,0:T(8,128)(2,1)S(1)}, bf16[2,8,32,256]{3,2,1,0:T(8,128)(2,1)S(1)}, u32[]{:S(2)}, u32[]{:S(2)}) collective-permute-start(bf16[2,8,32,256]{3,2,1,0:T(8,128)(2,1)S(1)} %pad_maximum_fusion.7), channel_id=1, source_target_pairs={{0,6},{1,7},{2,0},{3,1},{4,2},{5,3},{6,4},{7,5},{8,14},{9,15},{10,... | collective-permute-start | bytes 786440 | tf_op jit(solution)/shard_map/ppermute | solution.py:388
